TPU v7x, 1024 devices: a whole 8x8x8 slice. The times are simulated.
1024 devices in a mesh: exp: 32 (over y, z_hi, core), seq: 8 (over x), dp: 4 (over z_lo).
Axes of the slice: x: 8, y: 8, z: 8 (z_hi: 2, z_lo: 4; z = z_hi * 4 + z_lo), core: 2. Of those that a mesh axis runs over, the one named last changes fastest.
Arguments:
- queries: bfloat16 [32, 1024, 4, 2048], P('exp', None, 'dp', 'seq'), may hold values from -160 to 160
- latent_rows: bfloat16 [32, 1024, 512], P('exp'), may hold values from -8 to 8
- key_weight: bfloat16 [512, 4, 2048], P(None, 'dp', 'seq'), may hold values from -1 to 1
- output_grad: bfloat16 [32, 1024, 4, 2048], P('exp', 'seq', 'dp'), may hold values from -6 to 6
- down_weight: bfloat16 [32, 2048, 7168], P('exp', 'dp', 'seq'), may hold values from -0.125 to 0.125
- hidden_rows: bfloat16 [6144, 2048], P('exp', 'dp'), may hold values from -6 to 6
- upstream_rows: bfloat16 [6144, 7168], P('exp', 'seq'), may hold values from -6 to 6
- row_gates: float32 [6144], P('exp'), may hold values from 0.03 to 0.5
- row_counts: int32 [32, 3], P('exp'), may hold values from 0 to 64, as said below
Outputs:
- value_grad: bfloat16 [32, 1024, 4, 2048], P('exp', None, 'dp', 'seq')
- hidden_grad: float32 [6144, 2048], P(('exp', 'seq'), 'dp')
- weight_grad: bfloat16 [32, 2048, 7168], P('exp', 'dp', 'seq')
Inputs may be any that keep to these rules, and one draw needn't show every extreme that they name: `row_counts`: A block with 0 live rows means host j keeps no copy of expert e(j, b); in every draw some block is full with 64 live rows.
All inputs are finite; a program needn't handle non-finite values.
Results may differ from a plain program's by a relative error of at most 0.012.
The roundings to bfloat16 on the way count: a program that leaves them out, or rounds other values in their place, can miss the bound.
Values may be sent and summed in bfloat16 or wider, within the bound.
No kernel may reach another device: no remote copies, remote signals or barrier semaphores. Data moves between devices by JAX's collectives and lax.ppermute only.
A program may use at most 32 MiB of HBM per device.

v0:
```python
import math

import jax
import jax.numpy as jnp
from jax import lax
from jax.sharding import PartitionSpec as P

HEAD_DIM = 128


def shifted(block, axis, distance):
    devices = range(lax.axis_size(axis))
    route = [((i - distance) % len(devices), i) for i in devices]
    return lax.ppermute(block, axis, route)


def attend(queries, latent_rows, key_weight, head_grads):
    seq_len = queries.shape[1]
    feature_width = queries.shape[3]
    head_count = feature_width // HEAD_DIM
    key_rows = jnp.dot(
        latent_rows[0],
        key_weight.reshape(key_weight.shape[0], feature_width),
        preferred_element_type=jnp.float32,
    ).astype(jnp.bfloat16)
    key_heads = key_rows.reshape(seq_len, head_count, HEAD_DIM)
    query_heads = queries[0, :, 0, :].reshape(seq_len, head_count, HEAD_DIM)
    grad_heads = head_grads[0, :, 0, :].reshape(seq_len, head_count, HEAD_DIM)
    block_rows = max(min(512, seq_len), seq_len // 8)
    score_scale = 1.0 / math.sqrt(HEAD_DIM)
    accumulated = jnp.zeros((seq_len, head_count, HEAD_DIM), jnp.float32)
    for block_number in range(seq_len // block_rows):
        first_row = block_number * block_rows
        last_row = first_row + block_rows
        scores = (
            jnp.einsum(
                "qhd,khd->hqk",
                query_heads[first_row:last_row],
                key_heads[:last_row],
                preferred_element_type=jnp.float32,
            )
            * score_scale
        )
        allowed = jnp.arange(last_row)[None, :] <= (first_row + jnp.arange(block_rows))[:, None]
        scores = jnp.where(allowed[None], scores, -jnp.inf)
        row_max = jnp.max(scores, axis=2, keepdims=True)
        weights = jnp.exp(scores - row_max)
        softmax_rows = (weights / jnp.sum(weights, axis=2, keepdims=True)).astype(jnp.bfloat16)
        contribution = jnp.einsum(
            "hqk,qhd->khd",
            softmax_rows,
            grad_heads[first_row:last_row],
            preferred_element_type=jnp.float32,
        )
        accumulated = accumulated.at[:last_row].add(contribution)
    return accumulated.astype(jnp.bfloat16).reshape(1, seq_len, 1, feature_width)


def row_products(upstream, matrix):
    return jnp.einsum("rd,fd->rf", upstream, matrix, preferred_element_type=jnp.float32)


def term_product(scaled, upstream):
    return jnp.einsum("rf,rd->fd", scaled, upstream, preferred_element_type=jnp.float32).astype(
        jnp.bfloat16
    )


def expert_part(down_weight, hidden_rows, upstream_rows, row_gates, row_counts):
    own_tile = down_weight[0]
    capacity = hidden_rows.shape[0] // 3
    offset_step = lax.axis_size("exp") // 3
    live_rows = jnp.arange(capacity)[None, :] < row_counts[0][:, None]
    row_scale = jnp.where(live_rows, row_gates.reshape(3, capacity), 0.0).reshape(3 * capacity)
    scaled_rows = (row_scale[:, None] * hidden_rows.astype(jnp.float32)).astype(jnp.bfloat16)
    hidden_blocks = scaled_rows.reshape(3, capacity, scaled_rows.shape[1])
    upstream_blocks = upstream_rows.reshape(3, capacity, upstream_rows.shape[1])
    grad_blocks = [row_products(upstream_blocks[0], own_tile)]
    own_term = term_product(hidden_blocks[0], upstream_blocks[0])
    summed = lax.optimization_barrier(own_term).astype(jnp.float32)
    for block_index in (1, 2):
        replica_tile = shifted(down_weight, "exp", block_index * offset_step)[0]
        grad_blocks.append(row_products(upstream_blocks[block_index], replica_tile))
        block_term = term_product(hidden_blocks[block_index], upstream_blocks[block_index])
        summed = summed + shifted(block_term, "exp", -block_index * offset_step).astype(jnp.float32)
    grad_parts = jnp.concatenate(grad_blocks, 0) * row_scale[:, None]
    hidden_grad = lax.psum_scatter(grad_parts, "seq", scatter_dimension=0, tiled=True)
    weight_grad = summed.astype(jnp.bfloat16)[None]
    return (hidden_grad, weight_grad)


def on_device(
    queries,
    latent_rows,
    key_weight,
    output_grad,
    down_weight,
    hidden_rows,
    upstream_rows,
    row_gates,
    row_counts,
):
    head_grads = lax.all_to_all(output_grad, "seq", split_axis=3, concat_axis=1, tiled=True)
    hidden_grad, weight_grad = expert_part(
        down_weight, hidden_rows, upstream_rows, row_gates, row_counts
    )
    value_grad = attend(queries, latent_rows, key_weight, head_grads)
    return (value_grad, hidden_grad, weight_grad)


def solution(mesh):
    placed = (
        P("exp", None, "dp", "seq"),
        P("exp", None, None),
        P(None, "dp", "seq"),
        P("exp", "seq", "dp", None),
        P("exp", "dp", "seq"),
        P("exp", "dp"),
        P("exp", "seq"),
        P("exp"),
        P("exp", None),
    )
    return jax.shard_map(
        on_device,
        mesh=mesh,
        in_specs=placed,
        out_specs=(P("exp", None, "dp", "seq"), P(("exp", "seq"), "dp"), P("exp", "dp", "seq")),
        check_vma=False,
    )
```

profile of v0, /device:TPU:40, one launch (start us, length us, event | category | flops | bytes accessed | tf_op | source)
XLA Modules:
  0.0 173.1 jit_solution(4730463393306584338)
XLA Ops:
  7.2 5.9 %collective-permute-start.1 = (bf16[1,512,896]{2,1,0:T(8,128)(2,1)}, bf16[1,512,896]{2,1,0:T(8,128)(2,1)}, u32[]{:S(2)}, u32[]{:S(2)}) collective-permute-start(bf16[1,512,896]{2,1,0:T(8,128)(2,1)} %param.19), channel_id=1, source_target_pairs={{384,0},{416,32},{448,64},{480,96},{512,128},{544,160},{576,192},{... | collective-permute-start | bytes 2752520 | tf_op jit(solution)/shard_map/ppermute | solution.py:14
  13.0 14.2 %collective-permute-start = (bf16[1,512,896]{2,1,0:T(8,128)(2,1)}, bf16[1,512,896]{2,1,0:T(8,128)(2,1)}, u32[]{:S(2)}, u32[]{:S(2)}) collective-permute-start(bf16[1,512,896]{2,1,0:T(8,128)(2,1)} %param.19), channel_id=1, source_target_pairs={{704,0},{736,32},{768,64},{800,96},{832,128},{864,160},{896,192},{... | collective-permute-start | bytes 2752520 | tf_op jit(solution)/shard_map/ppermute | solution.py:14
  27.3 2.4 %copy.42 = bf16[1,128,1,2048]{1,2,0,3:T(2,128)(2,1)S(1)} copy(bf16[1,128,1,2048]{3,1,2,0:T(8,128)(2,1)} %param.18) | data formatting | bytes 1048576 | tf_op args[3]
  29.6 0.5 broadcast.99
  30.2 11.5 %reduce.4 = bf16[2048,128]{1,0:T(8,128)(2,1)S(1)} reduce(bf16[2048,1,1,128]{3,2,1,0:T(2,128)(2,1)S(1)} %bitcast.73, bf16[]{:T(256)} %broadcast.99), dimensions={1,2}, to_apply=%bitcast.56.reduce_sub_computation | reduce | bytes 1048578
  41.7 0.9 reshape.156
  42.6 7.3 %all-to-all-start = ((bf16[8,2,16384]{2,1,0:T(2,128)(2,1)}), bf16[8,2,16384]{2,1,0:T(2,128)(2,1)S(1)}, u32[]{:S(2)}, u32[]{:S(2)}) async-start(bf16[8,2,16384]{2,1,0:T(2,128)(2,1)} %reshape.156), calls=%async_computation | async-start | bytes 1048576 | tf_op jit(solution)/shard_map/all_to_all | solution.py:103
  49.9 0.8 iota_compare_fusion.1
  50.8 0.9 copy.58
  51.6 0.5 convolution_convert_fusion.3
  52.1 0.7 slice.113
  53.3 2.0 %fusion.47 = f32[2,512]{1,0:T(2,128)S(1)} fusion(pred[512,512]{0,1:T(8,128)(4,1)S(1)} %copy-done.4, bf16[512,2,128]{0,2,1:T(8,128)(2,1)} %bitcast.79, bf16[512,2,128]{0,2,1:T(8,128)(2,1)} %bitcast.77), kind=kOutput, calls=%fused_computation.62 | convolution fusion | flops 136315392 | bytes 790528 | tf_op jit(solution)/shard_map/sub | solution.py:47
  55.5 0.8 copy.59
  56.3 1.6 fusion.20
  57.9 4.6 %fusion.46 = (f32[2,512]{1,0:T(2,128)S(1)}, f32[2,512,1024]{1,2,0:T(8,128)}) fusion(pred[512,1024]{0,1:T(8,128)(4,1)S(1)} %iota_compare_fusion, bf16[1024,2,128]{0,2,1:T(8,128)(2,1)S(1)} %bitcast.75, bf16[512,2,128]{0,2,1:T(8,128)(2,1)} %bitcast.81), kind=kOutput, calls=%fused_computation.61 | convolution fusion | flops 272630784 | bytes 5509120 | tf_op jit(solution)/shard_map/sub | solution.py:47
  62.6 11.0 %collective-permute-done.1 = bf16[1,512,896]{2,1,0:T(8,128)(2,1)} collective-permute-done((bf16[1,512,896]{2,1,0:T(8,128)(2,1)}, bf16[1,512,896]{2,1,0:T(8,128)(2,1)}, u32[]{:S(2)}, u32[]{:S(2)}) %collective-permute-start.1) | collective-permute-done | bytes 917536 | tf_op jit(solution)/shard_map/ppermute | solution.py:14
  73.6 1.6 fusion.16
  75.1 14.5 %collective-permute-done = bf16[1,512,896]{2,1,0:T(8,128)(2,1)} collective-permute-done((bf16[1,512,896]{2,1,0:T(8,128)(2,1)}, bf16[1,512,896]{2,1,0:T(8,128)(2,1)}, u32[]{:S(2)}, u32[]{:S(2)}) %collective-permute-start) | collective-permute-done | bytes 917536 | tf_op jit(solution)/shard_map/ppermute | solution.py:14
  89.6 1.6 fusion.18
  91.2 0.9 multiply_convert_fusion
  92.1 1.3 convolution_convert_fusion.1
  93.4 1.3 convolution_convert_fusion
  94.7 0.5 reshape.157
  95.6 0.8 slice.102
  96.4 1.9 %collective-permute-start.2 = (bf16[512,896]{1,0:T(8,128)(2,1)}, bf16[512,896]{1,0:T(8,128)(2,1)S(1)}, u32[]{:S(2)}, u32[]{:S(2)}) collective-permute-start(bf16[512,896]{1,0:T(8,128)(2,1)} %convolution_convert_fusion.1), channel_id=1, source_target_pairs={{320,0},{352,32},{384,64},{416,96},{448,128},{480,160},{512,192},{... | collective-permute-start | bytes 2752520 | tf_op jit(solution)/shard_map/ppermute | solution.py:14
  98.3 4.7 %collective-permute-start.3 = (bf16[512,896]{1,0:T(8,128)(2,1)}, bf16[512,896]{1,0:T(8,128)(2,1)}, u32[]{:S(2)}, u32[]{:S(2)}) collective-permute-start(bf16[512,896]{1,0:T(8,128)(2,1)} %convolution_convert_fusion), channel_id=1, source_target_pairs={{640,0},{672,32},{704,64},{736,96},{768,128},{800,160},{832,192},{... | collective-permute-start | bytes 2752520 | tf_op jit(solution)/shard_map/ppermute | solution.py:14
  103.1 3.1 %convolution_bitcast_fusion = f32[512,2,128]{0,2,1:T(8,128)} fusion(bf16[512,2,128]{0,2,1:T(8,128)(2,1)} %slice.102, f32[2,512]{1,0:T(2,128)S(1)} %fusion.47, pred[512,512]{0,1:T(8,128)(4,1)S(1)} %copy-done.4, bf16[512,2,128]{0,2,1:T(8,128)(2,1)} %bitcast.80, bf16[512,2,128]{0,2,1:T(8,128)(2,1)S(1)} %bitcast.78), kind=kOutput, calls=%fused_computation.23 | convolution fusion | flops 271058432 | bytes 1576960 | tf_op jit(solution)/shard_map/hqk,qhd->khd/dot_general | solution.py:49
  106.6 3.1 %fusion.10 = bf16[1024,2,128]{0,2,1:T(8,128)(2,1)S(1)} fusion(bf16[512,2,128]{0,2,1:T(8,128)(2,1)S(1)} %slice.106, f32[2,512,1024]{1,2,0:T(8,128)} %get-tuple-element.54, f32[2,512]{1,0:T(2,128)S(1)} %get-tuple-element.53, f32[512,2,128]{0,2,1:T(8,128)} %convolution_bitcast_fusion), kind=kOutput, calls=%fused_computation.21 | convolution fusion | flops 271056896 | bytes 5509120 | tf_op jit(solution)/shard_map/hqk,qhd->khd/dot_general | solution.py:49
  109.7 1.0 copy.50
  111.2 43.0 %collective-permute-done.2 = bf16[512,896]{1,0:T(8,128)(2,1)S(1)} collective-permute-done((bf16[512,896]{1,0:T(8,128)(2,1)}, bf16[512,896]{1,0:T(8,128)(2,1)S(1)}, u32[]{:S(2)}, u32[]{:S(2)}) %collective-permute-start.2) | collective-permute-done | bytes 917536 | tf_op jit(solution)/shard_map/ppermute | solution.py:14
  154.1 9.7 %collective-permute-done.3 = bf16[512,896]{1,0:T(8,128)(2,1)} collective-permute-done((bf16[512,896]{1,0:T(8,128)(2,1)}, bf16[512,896]{1,0:T(8,128)(2,1)}, u32[]{:S(2)}, u32[]{:S(2)}) %collective-permute-start.3) | collective-permute-done | bytes 917536 | tf_op jit(solution)/shard_map/ppermute | solution.py:14
  163.8 2.4 %fusion.15 = bf16[1,512,896]{2,1,0:T(8,128)(2,1)} fusion(bf16[512,896]{1,0:T(8,128)(2,1)} %collective-permute-done.3, bf16[512,896]{1,0:T(8,128)(2,1)S(1)} %collective-permute-done.2, bf16[512,896]{1,0:T(8,128)(2,1)S(1)} %convolution_convert_fusion.2), kind=kLoop, calls=%fused_computation.29 | loop fusion | flops 2752512 | bytes 3670016 | tf_op jit(solution)/shard_map/broadcast_in_dim | solution.py:88
  (34 shorter events, 1.7 us)
Async XLA Ops:
  7.2 44.5 %copy-start = (bf16[1,1024,512]{2,1,0:T(8,128)(2,1)S(1)}, bf16[1,1024,512]{2,1,0:T(8,128)(2,1)}, u32[]{:S(2)}) copy-start(bf16[1,1024,512]{2,1,0:T(8,128)(2,1)} %param.16) | copy-start | bytes 3145732
  7.2 66.4 %collective-permute-start.1 = (bf16[1,512,896]{2,1,0:T(8,128)(2,1)}, bf16[1,512,896]{2,1,0:T(8,128)(2,1)}, u32[]{:S(2)}, u32[]{:S(2)}) collective-permute-start(bf16[1,512,896]{2,1,0:T(8,128)(2,1)} %param.19), channel_id=1, source_target_pairs={{384,0},{416,32},{448,64},{480,96},{512,128},{544,160},{576,192},{... | collective-permute-start | bytes 2752520 | tf_op jit(solution)/shard_map/ppermute | solution.py:14
  13.0 76.6 %collective-permute-start = (bf16[1,512,896]{2,1,0:T(8,128)(2,1)}, bf16[1,512,896]{2,1,0:T(8,128)(2,1)}, u32[]{:S(2)}, u32[]{:S(2)}) collective-permute-start(bf16[1,512,896]{2,1,0:T(8,128)(2,1)} %param.19), channel_id=1, source_target_pairs={{704,0},{736,32},{768,64},{800,96},{832,128},{864,160},{896,192},{... | collective-permute-start | bytes 2752520 | tf_op jit(solution)/shard_map/ppermute | solution.py:14
  29.6 21.1 %copy-start.2 = (bf16[1,1024,1,256]{3,1,2,0:T(8,128)(2,1)S(1)}, bf16[1,1024,1,256]{3,1,2,0:T(8,128)(2,1)}, u32[]{:S(2)}) copy-start(bf16[1,1024,1,256]{3,1,2,0:T(8,128)(2,1)} %param.15) | copy-start | bytes 1572868
  42.6 9.0 %copy-start.3 = (bf16[512,1,256]{2,0,1:T(8,128)(2,1)S(1)}, bf16[512,1,256]{2,0,1:T(8,128)(2,1)}, u32[]{:S(2)}) copy-start(bf16[512,1,256]{2,0,1:T(8,128)(2,1)} %param.17) | copy-start | bytes 786436
  42.6 52.1 %all-to-all-start = ((bf16[8,2,16384]{2,1,0:T(2,128)(2,1)}), bf16[8,2,16384]{2,1,0:T(2,128)(2,1)S(1)}, u32[]{:S(2)}, u32[]{:S(2)}) async-start(bf16[8,2,16384]{2,1,0:T(2,128)(2,1)} %reshape.156), calls=%async_computation | async-start | bytes 1048576 | tf_op jit(solution)/shard_map/all_to_all | solution.py:103
  49.9 116.3 %reduce-scatter.2.cloned.1.call-start = ((), (), s32[]{:S(2)}) async-start(), calls=%async_computation.2 | async-start | bytes 442368 | tf_op jit(solution)/shard_map/reduce_scatter | solution.py:87
  50.8 2.5 %copy-start.4 = (pred[512,512]{0,1:T(8,128)(4,1)S(1)}, pred[512,512]{0,1:T(8,128)(4,1)}, u32[]{:S(2)}) copy-start(pred[512,512]{0,1:T(8,128)(4,1)} %iota_compare_fusion.1) | copy-start | bytes 786436
  53.3 2.1 %copy-start.8 = (s32[1,3]{1,0:T(1,128)S(1)}, s32[1,3]{1,0:T(1,128)}, u32[]{:S(2)}) copy-start(s32[1,3]{1,0:T(1,128)} %param.23) | copy-start | bytes 40
  53.3 2.2 %copy-start.7 = (f32[192]{0:T(256)S(1)}, f32[192]{0:T(256)}, u32[]{:S(2)}) copy-start(f32[192]{0:T(256)} %param.22) | copy-start | bytes 2308
  53.3 3.1 %copy-start.1 = (bf16[192,896]{1,0:T(8,128)(2,1)S(1)}, bf16[192,896]{1,0:T(8,128)(2,1)}, u32[]{:S(2)}) copy-start(bf16[192,896]{1,0:T(8,128)(2,1)} %param.21) | copy-start | bytes 1032196
  62.6 28.6 %copy-start.6 = (bf16[192,512]{1,0:T(8,128)(2,1)S(1)}, bf16[192,512]{1,0:T(8,128)(2,1)}, u32[]{:S(2)}) copy-start(bf16[192,512]{1,0:T(8,128)(2,1)} %param.20) | copy-start | bytes 589828
  95.4 7.8 %copy-start.5 = (bf16[1,512,1,256]{1,3,2,0:T(8,128)(2,1)S(1)}, bf16[1,512,1,256]{1,3,2,0:T(8,128)(2,1)}, u32[]{:S(2)}) copy-start(bf16[1,512,1,256]{1,3,2,0:T(8,128)(2,1)} %copy.58) | copy-start | bytes 786436
  96.4 57.7 %collective-permute-start.2 = (bf16[512,896]{1,0:T(8,128)(2,1)}, bf16[512,896]{1,0:T(8,128)(2,1)S(1)}, u32[]{:S(2)}, u32[]{:S(2)}) collective-permute-start(bf16[512,896]{1,0:T(8,128)(2,1)} %convolution_convert_fusion.1), channel_id=1, source_target_pairs={{320,0},{352,32},{384,64},{416,96},{448,128},{480,160},{512,192},{... | collective-permute-start | bytes 2752520 | tf_op jit(solution)/shard_map/ppermute | solution.py:14
  98.3 65.5 %collective-permute-start.3 = (bf16[512,896]{1,0:T(8,128)(2,1)}, bf16[512,896]{1,0:T(8,128)(2,1)}, u32[]{:S(2)}, u32[]{:S(2)}) collective-permute-start(bf16[512,896]{1,0:T(8,128)(2,1)} %convolution_convert_fusion), channel_id=1, source_target_pairs={{640,0},{672,32},{704,64},{736,96},{768,128},{800,160},{832,192},{... | collective-permute-start | bytes 2752520 | tf_op jit(solution)/shard_map/ppermute | solution.py:14
Sparse Core Ops, SparseCore 0:
  103.2 41.9 reduce-scatter.1
where the time goes:
time: 174 us; the launch traced here: 173 us
  waiting for transfers between devices  78.2 us (45%)
  starting transfers between devices  34.1 us (20%)
  matrix products  21.2 us (12%)
  other arithmetic  16.1 us (9%)
  between operations  14.3 us (8%)
  local copies, waits for them, and re-layouts  9.33 us (5%)
    ppermute x4, waiting for transfers between devices, shifted(): return lax.ppermute(block, axis, route)  78.1 us
    ppermute x4, starting transfers between devices, shifted(): return lax.ppermute(block, axis, route)  26.7 us
    unnamed x1, other arithmetic  11.5 us
    all_to_all x1, starting transfers between devices, on_device(): lax.all_to_all(output_grad, 'seq', split_axis=3, concat_axis=1, tiled=True)  7.34 us
    unnamed x26, local copies, waits for them, and re-layouts  7.13 us
    sub x2, matrix products, attend(): weights = jnp.exp(scores - row_max)  6.67 us
    dot_general x2, matrix products, attend(): jnp.einsum('hqk,qhd->khd', softmax_rows, grad_heads[first_row:last_row],...  6.27 us
    dot_general x3, matrix products, row_products(): jnp.einsum('rd,fd->rf', upstream, matrix, preferred_element_type=jnp.floa...  4.71 us
  transfers between devices with their start and end apart: 6, of which 4 were waited for; matrix products, arithmetic and copies ran while one was open for 26% of the time, Pallas kernels for 0%

commit v1 on v0

v1 whole, which is shorter than its diff:
```python
import math

import jax
import jax.numpy as jnp
from jax import lax
from jax.experimental import pallas as pl
from jax.experimental.pallas import tpu as pltpu
from jax.sharding import PartitionSpec as P


HEAD_DIM = 128
TILE = 256
NT = (((1,), (1,)), ((), ()))
TN = (((0,), (0,)), ((), ()))
VMEM = pl.BlockSpec(memory_space=pltpu.VMEM)
SMEM = pl.BlockSpec(memory_space=pltpu.SMEM)


def call(body, shapes, specs, **options):
    single = not isinstance(shapes, (list, tuple))
    return pl.pallas_call(
        body,
        out_shape=shapes,
        in_specs=specs,
        out_specs=VMEM if single else tuple(VMEM for _ in shapes),
        compiler_params=pltpu.CompilerParams(vmem_limit_bytes=48 * 1024 * 1024),
        **options,
    )


def pack_body(counts, gates, hidden, upstream, pack1, pack2, own, scales):
    cap = own.shape[0]
    wide = upstream.shape[1]
    rows = lax.broadcasted_iota(jnp.int32, (cap, cap), 0)
    cols = lax.broadcasted_iota(jnp.int32, (cap, cap), 1)
    outs = (None, pack1, pack2)
    for b in range(3):
        gate = gates[0:1, b * cap : (b + 1) * cap]
        chosen = jnp.where((rows == cols) & (rows < counts[0, b]), gate, 0.0)
        scale = jnp.sum(chosen, axis=1, keepdims=True)
        span = slice(b * cap, (b + 1) * cap)
        scaled = (scale * hidden[span, :].astype(jnp.float32)).astype(jnp.bfloat16)
        scales[span, :] = jnp.broadcast_to(scale, (cap, 128))
        if b == 0:
            own[...] = scaled
        else:
            outs[b][:, :wide] = upstream[span, :]
            outs[b][:, wide:] = scaled


def split_body(grads, pieces):
    count, _, width = pieces.shape
    for s in range(count):
        pieces[s] = grads[:, s * width : (s + 1) * width]


def probs_body(latent, key_weight, queries, probs, keys):
    seq_len = latent.shape[0]
    keys[...] = jnp.dot(
        latent[...], key_weight[...], preferred_element_type=jnp.float32
    ).astype(jnp.bfloat16)
    factor = math.log2(math.e) / math.sqrt(HEAD_DIM)
    later = lax.broadcasted_iota(jnp.int32, (TILE, TILE), 0) > lax.broadcasted_iota(
        jnp.int32, (TILE, TILE), 1
    )
    for head in range(queries.shape[1] // HEAD_DIM):
        feats = slice(head * HEAD_DIM, (head + 1) * HEAD_DIM)
        for tile in range(seq_len // TILE):
            start, stop = tile * TILE, (tile + 1) * TILE
            query = queries[start:stop, feats]
            diagonal = lax.dot_general(
                keys[start:stop, feats], query, NT, preferred_element_type=jnp.float32
            )
            diagonal = jnp.where(later, -jnp.inf, diagonal)
            top = jnp.max(diagonal, axis=0, keepdims=True)
            if tile:
                before = lax.dot_general(
                    keys[:start, feats], query, NT, preferred_element_type=jnp.float32
                )
                top = jnp.maximum(top, jnp.max(before, axis=0, keepdims=True))
                before = jnp.exp2((before - top) * factor)
            diagonal = jnp.exp2((diagonal - top) * factor)
            total = jnp.sum(diagonal, axis=0, keepdims=True)
            if tile:
                total = total + jnp.sum(before, axis=0, keepdims=True)
            inverse = 1.0 / total
            probs[head, start:stop, start:stop] = (diagonal * inverse).astype(jnp.bfloat16)
            if tile:
                probs[head, :start, start:stop] = (before * inverse).astype(jnp.bfloat16)


def value_body(probs, grads, out):
    seq_len = grads.shape[0]
    for head in range(grads.shape[1] // HEAD_DIM):
        feats = slice(head * HEAD_DIM, (head + 1) * HEAD_DIM)
        for tile in range(seq_len // TILE):
            start, stop = tile * TILE, (tile + 1) * TILE
            out[start:stop, feats] = jnp.dot(
                probs[head, start:stop, start:],
                grads[start:, feats],
                preferred_element_type=jnp.float32,
            ).astype(jnp.bfloat16)


def partial_body(weight, upstream, first, second, out):
    cap = first.shape[0]
    wide = weight.shape[1]
    matrix = weight[...]
    for b, rows in enumerate((upstream[:cap, :], first[:, :wide], second[:, :wide])):
        out[b * cap : (b + 1) * cap, :] = lax.dot_general(
            rows, matrix, NT, preferred_element_type=jnp.float32
        ).astype(jnp.bfloat16)


def weight_body(upstream, own, first, second, out):
    cap, hid = own.shape
    wide = upstream.shape[1]
    chunk = 128
    for start in range(0, hid, chunk):
        stop = start + chunk
        total = None
        for left, right in (
            (own[:, start:stop], upstream[:cap, :]),
            (first[:, wide + start : wide + stop], first[:, :wide]),
            (second[:, wide + start : wide + stop], second[:, :wide]),
        ):
            term = lax.dot_general(left, right, TN, preferred_element_type=jnp.float32)
            term = term.astype(jnp.bfloat16).astype(jnp.float32)
            total = term if total is None else total + term
        out[start:stop, :] = total.astype(jnp.bfloat16)


def shifted(block, axis, distance):
    devices = range(lax.axis_size(axis))
    route = [(i, (i + distance) % len(devices)) for i in devices]
    return lax.ppermute(block, axis, route)


def on_device(
    queries,
    latent_rows,
    key_weight,
    output_grad,
    down_weight,
    hidden_rows,
    upstream_rows,
    row_gates,
    row_counts,
):
    n_seq = lax.axis_size("seq")
    n_exp = lax.axis_size("exp")
    step = n_exp // 3
    rows, hid = hidden_rows.shape
    cap = rows // 3
    own_rows = rows // n_seq
    wide = upstream_rows.shape[1]
    seq_len, width = queries.shape[1], queries.shape[3]
    tokens = output_grad.shape[1]
    bf16, f32 = jnp.bfloat16, jnp.float32

    pack1, pack2, own, scales = call(
        pack_body,
        [
            jax.ShapeDtypeStruct((cap, wide + hid), bf16),
            jax.ShapeDtypeStruct((cap, wide + hid), bf16),
            jax.ShapeDtypeStruct((cap, hid), bf16),
            jax.ShapeDtypeStruct((rows, 128), f32),
        ],
        [SMEM, VMEM, VMEM, VMEM],
        name="pack",
    )(row_counts, row_gates.reshape(1, rows), hidden_rows, upstream_rows)
    first = shifted(pack1, "exp", -step)
    second = shifted(pack2, "exp", -2 * step)

    pack1, pack2, output_grad = lax.optimization_barrier((pack1, pack2, output_grad))
    pieces = call(
        split_body, jax.ShapeDtypeStruct((n_seq, tokens, width), bf16), [VMEM], name="split"
    )(output_grad.reshape(tokens, n_seq * width))
    head_grads = lax.all_to_all(pieces, "seq", split_axis=0, concat_axis=0, tiled=True)

    probs = call(
        probs_body,
        jax.ShapeDtypeStruct((width // HEAD_DIM, seq_len, seq_len), bf16),
        [VMEM, VMEM, VMEM],
        scratch_shapes=[pltpu.VMEM((seq_len, width), bf16)],
        name="probs",
    )(
        latent_rows[0],
        key_weight.reshape(key_weight.shape[0], width),
        queries.reshape(seq_len, width),
    )

    first, second, head_grads, probs = lax.optimization_barrier(
        (first, second, head_grads, probs)
    )
    parts = call(
        partial_body, jax.ShapeDtypeStruct((rows, hid), bf16), [VMEM] * 4, name="parts"
    )(down_weight[0], upstream_rows, first, second)
    shares = lax.all_to_all(
        parts.reshape(n_seq, own_rows, hid), "seq", split_axis=0, concat_axis=0, tiled=True
    )

    weight_grad = call(
        weight_body, jax.ShapeDtypeStruct((hid, wide), bf16), [VMEM] * 4, name="weight"
    )(upstream_rows, own, first, second)[None]
    value_grad = call(
        value_body, jax.ShapeDtypeStruct((seq_len, width), bf16), [VMEM] * 2, name="value"
    )(probs, head_grads.reshape(seq_len, width)).reshape(queries.shape)

    shares, weight_grad = lax.optimization_barrier((shares, weight_grad))

    summed = jnp.sum(shares.astype(f32), axis=0)
    needs = [
        [b for b in (1, 2) if s * own_rows < (b + 1) * cap and (s + 1) * own_rows > b * cap]
        for s in range(n_seq)
    ]
    backs = []
    for turn in range(2):
        route = [
            (e * n_seq + s, (e + blocks[turn] * step) % n_exp * n_seq + s)
            for s, blocks in enumerate(needs)
            if turn < len(blocks)
            for e in range(n_exp)
        ]
        backs.append(lax.ppermute(summed, ("exp", "seq"), route))
    row_start = lax.axis_index("seq") * own_rows
    block_ids = ((row_start + jnp.arange(own_rows)) // cap)[:, None]
    second_of_two = (block_ids == 2) & (row_start // cap == 1)
    total = jnp.where(block_ids == 0, summed, jnp.where(second_of_two, backs[1], backs[0]))
    own_scale = lax.dynamic_slice(scales, (row_start, 0), (own_rows, 1))
    hidden_grad = total * own_scale
    return (value_grad, hidden_grad, weight_grad)


def solution(mesh):
    placed = (
        P("exp", None, "dp", "seq"),
        P("exp", None, None),
        P(None, "dp", "seq"),
        P("exp", "seq", "dp", None),
        P("exp", "dp", "seq"),
        P("exp", "dp"),
        P("exp", "seq"),
        P("exp"),
        P("exp", None),
    )
    return jax.shard_map(
        on_device,
        mesh=mesh,
        in_specs=placed,
        out_specs=(P("exp", None, "dp", "seq"), P(("exp", "seq"), "dp"), P("exp", "dp", "seq")),
        check_vma=False,
    )
```

time: 174 us -> 82.4 us (0.47)
  the two profiles are of different devices: /device:TPU:40 before, /device:TPU:4 now
where the time goes in v1:
time: 82.4 us; the launch traced here: 81.8 us
  starting transfers between devices  39.1 us (47%)
  waiting for transfers between devices  20.2 us (25%)
  local copies, waits for them, and re-layouts  11.9 us (14%)
  Pallas kernels  9.16 us (11%)
    all_to_all x1, starting transfers between devices, on_device(): lax.all_to_all(pieces, 'seq', split_axis=0, concat_axis=0, tiled=True)  16.5 us
    ppermute x2, starting transfers between devices, shifted(): return lax.ppermute(block, axis, route)  12.2 us
    unnamed x24, local copies, waits for them, and re-layouts  11.7 us
    ppermute x2, waiting for transfers between devices, shifted(): return lax.ppermute(block, axis, route)  7.97 us
    all_to_all x1, starting transfers between devices, on_device(): lax.all_to_all(parts.reshape(n_seq, own_rows, hid), 'seq', split_axis=0,...  7.2 us
    ppermute x2, waiting for transfers between devices, on_device(): backs.append(lax.ppermute(summed, ('exp', 'seq'), route))  6.71 us
    all_to_all x1, waiting for transfers between devices, on_device(): lax.all_to_all(parts.reshape(n_seq, own_rows, hid), 'seq', split_axis=0,...  5.52 us
    ppermute x2, starting transfers between devices, on_device(): backs.append(lax.ppermute(summed, ('exp', 'seq'), route))  3.12 us
  transfers between devices with their start and end apart: 6, of which 4 were waited for; matrix products, arithmetic and copies ran while one was open for 0% of the time, Pallas kernels for 7%

profile of v1, /device:TPU:4, one launch (start us, length us, event | category | flops | bytes accessed | tf_op | source)
XLA Modules:
  0.0 81.8 jit_solution(1856468957194900262)
XLA Ops:
  0.6 0.0 copy-start.2
  0.6 1.0 %copy-done.2 = bf16[192,896]{1,0:T(8,128)(2,1)S(1)} copy-done((bf16[192,896]{1,0:T(8,128)(2,1)S(1)}, bf16[192,896]{1,0:T(8,128)(2,1)}, u32[]{:S(2)}) %copy-start.2) | copy-done | bytes 344088
  1.6 0.9 %copy-done.9 = bf16[192,512]{1,0:T(8,128)(2,1)S(1)} copy-done((bf16[192,512]{1,0:T(8,128)(2,1)S(1)}, bf16[192,512]{1,0:T(8,128)(2,1)}, u32[]{:S(2)}) %copy-start.9) | copy-done | bytes 196632
  2.5 0.7 copy-done.10
  3.2 0.7 copy-done.11
  3.9 0.7 pack.1
  4.6 0.0 copy-start.3
  4.6 0.0 copy-start.5
  4.6 1.1 %copy-done.7 = bf16[1,128,1,2048]{3,1,2,0:T(8,128)(2,1)S(1)} copy-done((bf16[1,128,1,2048]{3,1,2,0:T(8,128)(2,1)S(1)}, bf16[1,128,1,2048]{3,1,2,0:T(8,128)(2,1)}, u32[]{:S(2)}) %copy-start.7) | copy-done | bytes 524312
  5.7 0.8 %split.1 = bf16[8,128,256]{2,1,0:T(8,128)(2,1)} custom-call(bf16[128,2048]{1,0:T(8,128)(2,1)S(1)} %bitcast.14), custom_call_target="tpu_custom_call" | custom-call | tf_op jit(solution)/shard_map/split/pallas_call | solution.py:176
  6.6 16.5 %all-to-all-start = ((bf16[8,128,256]{2,1,0:T(8,128)(2,1)}), bf16[8,128,256]{2,1,0:T(8,128)(2,1)S(1)}, u32[]{:S(2)}, u32[]{:S(2)}) async-start(bf16[8,128,256]{2,1,0:T(8,128)(2,1)} %split.1), calls=%async_computation | async-start | bytes 1048576 | tf_op jit(solution)/shard_map/all_to_all | solution.py:179
  23.1 10.3 %collective-permute-start = (bf16[64,1408]{1,0:T(8,128)(2,1)S(1)}, bf16[64,1408]{1,0:T(8,128)(2,1)S(1)}, u32[]{:S(2)}, u32[]{:S(2)}) collective-permute-start(bf16[64,1408]{1,0:T(8,128)(2,1)S(1)} %get-tuple-element.14), channel_id=1, source_target_pairs={{0,704},{32,736},{64,768},{96,800},{128,832},{160,864},{192,896},{... | collective-permute-start | bytes 540680 | tf_op jit(solution)/shard_map/ppermute | solution.py:136
  33.4 1.9 %collective-permute-start.1 = (bf16[64,1408]{1,0:T(8,128)(2,1)S(1)}, bf16[64,1408]{1,0:T(8,128)(2,1)S(1)}, u32[]{:S(2)}, u32[]{:S(2)}) collective-permute-start(bf16[64,1408]{1,0:T(8,128)(2,1)S(1)} %get-tuple-element.15), channel_id=1, source_target_pairs={{0,384},{32,416},{64,448},{96,480},{128,512},{160,544},{192,576},{... | collective-permute-start | bytes 540680 | tf_op jit(solution)/shard_map/ppermute | solution.py:136
  35.4 0.0 copy-start.4
  35.4 1.2 %copy-done.4 = bf16[1,1024,512]{2,1,0:T(8,128)(2,1)S(1)} copy-done((bf16[1,1024,512]{2,1,0:T(8,128)(2,1)S(1)}, bf16[1,1024,512]{2,1,0:T(8,128)(2,1)}, u32[]{:S(2)}) %copy-start.4) | copy-done | bytes 1048600
  36.6 1.0 %copy-done.6 = bf16[1,1024,1,256]{3,1,2,0:T(8,128)(2,1)S(1)} copy-done((bf16[1,1024,1,256]{3,1,2,0:T(8,128)(2,1)S(1)}, bf16[1,1024,1,256]{3,1,2,0:T(8,128)(2,1)}, u32[]{:S(2)}) %copy-start.6) | copy-done | bytes 524312
  37.6 0.9 %copy-done.8 = bf16[512,1,256]{2,0,1:T(8,128)(2,1)S(1)} copy-done((bf16[512,1,256]{2,0,1:T(8,128)(2,1)S(1)}, bf16[512,1,256]{2,0,1:T(8,128)(2,1)}, u32[]{:S(2)}) %copy-start.8) | copy-done | bytes 262168
  38.6 2.5 %probs.1 = bf16[2,1024,1024]{2,1,0:T(8,128)(2,1)S(1)} custom-call(bf16[1024,512]{1,0:T(8,128)(2,1)S(1)} %bitcast.11, bf16[512,256]{1,0:T(8,128)(2,1)S(1)} %bitcast.15, bf16[1024,256]{1,0:T(8,128)(2,1)S(1)} %bitcast.13), custom_call_target="tpu_custom_call" | custom-call | tf_op jit(solution)/shard_map/probs/pallas_call | solution.py:181
  41.1 2.0 %copy-done = bf16[2,1024,1024]{2,1,0:T(8,128)(2,1)} copy-done((bf16[2,1024,1024]{2,1,0:T(8,128)(2,1)}, bf16[2,1024,1024]{2,1,0:T(8,128)(2,1)S(1)}, u32[]{:S(2)}) %copy-start) | copy-done | bytes 4194328
  43.1 1.3 %collective-permute-done.first = bf16[64,1408]{1,0:T(8,128)(2,1)S(1)} collective-permute-done((bf16[64,1408]{1,0:T(8,128)(2,1)S(1)}, bf16[64,1408]{1,0:T(8,128)(2,1)S(1)}, u32[]{:S(2)}, u32[]{:S(2)}) %collective-permute-start) | collective-permute-done | bytes 180256 | tf_op jit(solution)/shard_map/ppermute | solution.py:136
  44.4 6.6 %collective-permute-done.1.second = bf16[64,1408]{1,0:T(8,128)(2,1)S(1)} collective-permute-done((bf16[64,1408]{1,0:T(8,128)(2,1)S(1)}, bf16[64,1408]{1,0:T(8,128)(2,1)S(1)}, u32[]{:S(2)}, u32[]{:S(2)}) %collective-permute-start.1) | collective-permute-done | bytes 180256 | tf_op jit(solution)/shard_map/ppermute | solution.py:136
  51.1 1.6 %parts.1 = bf16[192,512]{1,0:T(8,128)(2,1)} custom-call(bf16[512,896]{1,0:T(8,128)(2,1)S(1)} %bitcast.12, bf16[192,896]{1,0:T(8,128)(2,1)S(1)} %copy-done.3, bf16[64,1408]{1,0:T(8,128)(2,1)S(1)} %collective-permute-done.first, bf16[64,1408]{1,0:T(8,128)(2,1)S(1)} %collective-permute-done.1.second), custom_call_target="tpu_custom_call" | custom-call | tf_op jit(solution)/shard_map/parts/pallas_call | solution.py:196
  52.7 7.2 %all-to-all-start.1 = ((bf16[8,24,512]{2,1,0:T(8,128)(2,1)}), bf16[8,24,512]{2,1,0:T(8,128)(2,1)S(1)}, u32[]{:S(2)}, u32[]{:S(2)}) async-start(bf16[8,24,512]{2,1,0:T(8,128)(2,1)} %bitcast.8), calls=%async_computation.1 | async-start | bytes 393216 | tf_op jit(solution)/shard_map/all_to_all | solution.py:199
  59.9 1.8 %weight.1 = bf16[512,896]{1,0:T(8,128)(2,1)} custom-call(bf16[192,896]{1,0:T(8,128)(2,1)S(1)} %copy-done.3, bf16[64,512]{1,0:T(8,128)(2,1)S(1)} %get-tuple-element.21.own, bf16[64,1408]{1,0:T(8,128)(2,1)S(1)} %collective-permute-done.first, bf16[64,1408]{1,0:T(8,128)(2,1)S(1)} %collective-permute-done.1.second), custom_call_target="tpu_custom_call" | custom-call | tf_op jit(solution)/shard_map/weight/pallas_call | solution.py:203
  61.7 5.5 %all-to-all-done.1 = bf16[8,24,512]{2,1,0:T(8,128)(2,1)S(1)} async-done(((bf16[8,24,512]{2,1,0:T(8,128)(2,1)}), bf16[8,24,512]{2,1,0:T(8,128)(2,1)S(1)}, u32[]{:S(2)}, u32[]{:S(2)}) %all-to-all-start.1) | async-done | bytes 196640 | tf_op jit(solution)/shard_map/all_to_all | solution.py:199
  67.3 2.5 %collective-permute-start.3 = (f32[24,512]{1,0:T(8,128)S(1)}, f32[24,512]{1,0:T(8,128)S(1)}, u32[]{:S(2)}, u32[]{:S(2)}) collective-permute-start(f32[24,512]{1,0:T(8,128)S(1)} %convert_reduce_fusion), channel_id=1, source_target_pairs={{8,328},{40,360},{72,392},{104,424},{136,456},{168,488},{200,520},... | collective-permute-start | bytes 147464 | tf_op jit(solution)/shard_map/ppermute | solution.py:225
  69.8 0.7 collective-permute-start.2
  70.5 0.1 dynamic-slice_reduce_fusion
  70.6 2.2 %copy-done.1 = bf16[2,1024,1024]{2,1,0:T(8,128)(2,1)S(1)} copy-done((bf16[2,1024,1024]{2,1,0:T(8,128)(2,1)S(1)}, bf16[2,1024,1024]{2,1,0:T(8,128)(2,1)}, u32[]{:S(2)}) %copy-start.1) | copy-done | bytes 4194328
  72.8 1.6 %value.1 = bf16[1024,256]{1,0:T(8,128)(2,1)} custom-call(bf16[2,1024,1024]{2,1,0:T(8,128)(2,1)S(1)} %copy-done.1, bf16[1024,256]{1,0:T(8,128)(2,1)S(1)} %bitcast.10), custom_call_target="tpu_custom_call" | custom-call | tf_op jit(solution)/shard_map/value/pallas_call | solution.py:206
  74.4 6.7 %collective-permute-done.3 = f32[24,512]{1,0:T(8,128)S(1)} collective-permute-done((f32[24,512]{1,0:T(8,128)S(1)}, f32[24,512]{1,0:T(8,128)S(1)}, u32[]{:S(2)}, u32[]{:S(2)}) %collective-permute-start.3) | collective-permute-done | bytes 49184 | tf_op jit(solution)/shard_map/ppermute | solution.py:225
  81.1 0.7 select_multiply_fusion
  (14 shorter events, 0.1 us)
Async XLA Ops:
  0.6 1.0 %copy-start.2 = (bf16[192,896]{1,0:T(8,128)(2,1)S(1)}, bf16[192,896]{1,0:T(8,128)(2,1)}, u32[]{:S(2)}) copy-start(bf16[192,896]{1,0:T(8,128)(2,1)} %upstream.5) | copy-start | bytes 1032196
  1.6 0.9 %copy-start.9 = (bf16[192,512]{1,0:T(8,128)(2,1)S(1)}, bf16[192,512]{1,0:T(8,128)(2,1)}, u32[]{:S(2)}) copy-start(bf16[192,512]{1,0:T(8,128)(2,1)} %hidden.1) | copy-start | bytes 589828
  2.5 0.7 copy-start.10
  3.2 0.7 copy-start.11
  4.6 46.5 %copy-start.3 = (bf16[192,896]{1,0:T(8,128)(2,1)S(1)}, bf16[192,896]{1,0:T(8,128)(2,1)}, u32[]{:S(2)}) copy-start(bf16[192,896]{1,0:T(8,128)(2,1)} %upstream.5) | copy-start | bytes 1032196
  4.6 46.5 %copy-start.5 = (bf16[1,512,896]{2,1,0:T(8,128)(2,1)S(1)}, bf16[1,512,896]{2,1,0:T(8,128)(2,1)}, u32[]{:S(2)}) copy-start(bf16[1,512,896]{2,1,0:T(8,128)(2,1)} %param.13) | copy-start | bytes 2752516
  4.6 1.1 %copy-start.7 = (bf16[1,128,1,2048]{3,1,2,0:T(8,128)(2,1)S(1)}, bf16[1,128,1,2048]{3,1,2,0:T(8,128)(2,1)}, u32[]{:S(2)}) copy-start(bf16[1,128,1,2048]{3,1,2,0:T(8,128)(2,1)} %param.12) | copy-start | bytes 1572868
  6.6 44.5 %all-to-all-start = ((bf16[8,128,256]{2,1,0:T(8,128)(2,1)}), bf16[8,128,256]{2,1,0:T(8,128)(2,1)S(1)}, u32[]{:S(2)}, u32[]{:S(2)}) async-start(bf16[8,128,256]{2,1,0:T(8,128)(2,1)} %split.1), calls=%async_computation | async-start | bytes 1048576 | tf_op jit(solution)/shard_map/all_to_all | solution.py:179
  23.1 21.3 %collective-permute-start = (bf16[64,1408]{1,0:T(8,128)(2,1)S(1)}, bf16[64,1408]{1,0:T(8,128)(2,1)S(1)}, u32[]{:S(2)}, u32[]{:S(2)}) collective-permute-start(bf16[64,1408]{1,0:T(8,128)(2,1)S(1)} %get-tuple-element.14), channel_id=1, source_target_pairs={{0,704},{32,736},{64,768},{96,800},{128,832},{160,864},{192,896},{... | collective-permute-start | bytes 540680 | tf_op jit(solution)/shard_map/ppermute | solution.py:136
  33.4 17.6 %collective-permute-start.1 = (bf16[64,1408]{1,0:T(8,128)(2,1)S(1)}, bf16[64,1408]{1,0:T(8,128)(2,1)S(1)}, u32[]{:S(2)}, u32[]{:S(2)}) collective-permute-start(bf16[64,1408]{1,0:T(8,128)(2,1)S(1)} %get-tuple-element.15), channel_id=1, source_target_pairs={{0,384},{32,416},{64,448},{96,480},{128,512},{160,544},{192,576},{... | collective-permute-start | bytes 540680 | tf_op jit(solution)/shard_map/ppermute | solution.py:136
  35.4 1.2 %copy-start.4 = (bf16[1,1024,512]{2,1,0:T(8,128)(2,1)S(1)}, bf16[1,1024,512]{2,1,0:T(8,128)(2,1)}, u32[]{:S(2)}) copy-start(bf16[1,1024,512]{2,1,0:T(8,128)(2,1)} %param.10) | copy-start | bytes 3145732
  36.6 1.0 %copy-start.6 = (bf16[1,1024,1,256]{3,1,2,0:T(8,128)(2,1)S(1)}, bf16[1,1024,1,256]{3,1,2,0:T(8,128)(2,1)}, u32[]{:S(2)}) copy-start(bf16[1,1024,1,256]{3,1,2,0:T(8,128)(2,1)} %param.9) | copy-start | bytes 1572868
  37.6 0.9 %copy-start.8 = (bf16[512,1,256]{2,0,1:T(8,128)(2,1)S(1)}, bf16[512,1,256]{2,0,1:T(8,128)(2,1)}, u32[]{:S(2)}) copy-start(bf16[512,1,256]{2,0,1:T(8,128)(2,1)} %param.11) | copy-start | bytes 786436
  41.1 2.0 %copy-start = (bf16[2,1024,1024]{2,1,0:T(8,128)(2,1)}, bf16[2,1024,1024]{2,1,0:T(8,128)(2,1)S(1)}, u32[]{:S(2)}) copy-start(bf16[2,1024,1024]{2,1,0:T(8,128)(2,1)S(1)} %probs.1) | copy-start | bytes 12582916
  52.7 14.6 %all-to-all-start.1 = ((bf16[8,24,512]{2,1,0:T(8,128)(2,1)}), bf16[8,24,512]{2,1,0:T(8,128)(2,1)S(1)}, u32[]{:S(2)}, u32[]{:S(2)}) async-start(bf16[8,24,512]{2,1,0:T(8,128)(2,1)} %bitcast.8), calls=%async_computation.1 | async-start | bytes 393216 | tf_op jit(solution)/shard_map/all_to_all | solution.py:199
  67.3 13.8 %collective-permute-start.3 = (f32[24,512]{1,0:T(8,128)S(1)}, f32[24,512]{1,0:T(8,128)S(1)}, u32[]{:S(2)}, u32[]{:S(2)}) collective-permute-start(f32[24,512]{1,0:T(8,128)S(1)} %convert_reduce_fusion), channel_id=1, source_target_pairs={{8,328},{40,360},{72,392},{104,424},{136,456},{168,488},{200,520},... | collective-permute-start | bytes 147464 | tf_op jit(solution)/shard_map/ppermute | solution.py:225
  69.8 11.3 %collective-permute-start.2 = (f32[24,512]{1,0:T(8,128)S(1)}, f32[24,512]{1,0:T(8,128)S(1)}, u32[]{:S(2)}, u32[]{:S(2)}) collective-permute-start(f32[24,512]{1,0:T(8,128)S(1)} %convert_reduce_fusion), channel_id=1, source_target_pairs={{20,660},{52,692},{84,724},{116,756},{148,788},{180,820},{212,852}... | collective-permute-start | bytes 147464 | tf_op jit(solution)/shard_map/ppermute | solution.py:225
  70.6 2.2 %copy-start.1 = (bf16[2,1024,1024]{2,1,0:T(8,128)(2,1)S(1)}, bf16[2,1024,1024]{2,1,0:T(8,128)(2,1)}, u32[]{:S(2)}) copy-start(bf16[2,1024,1024]{2,1,0:T(8,128)(2,1)} %copy-done) | copy-start | bytes 12582916

commit v2 on v1

v2 whole, which is shorter than its diff:
```python
import math

import jax
import jax.numpy as jnp
from jax import lax
from jax.experimental import pallas as pl
from jax.experimental.pallas import tpu as pltpu
from jax.sharding import PartitionSpec as P


HEAD_DIM = 128
TILE = 256
NT = (((1,), (1,)), ((), ()))
TN = (((0,), (0,)), ((), ()))
VMEM = pl.BlockSpec(memory_space=pltpu.VMEM)
HBM = pl.BlockSpec(memory_space=pltpu.HBM)


def call(body, shapes, specs, outs=VMEM, limit=12, **options):
    single = not isinstance(shapes, (list, tuple))
    return pl.pallas_call(
        body,
        out_shape=shapes,
        in_specs=specs,
        out_specs=outs if single else tuple(outs for _ in shapes),
        compiler_params=pltpu.CompilerParams(vmem_limit_bytes=limit * 1024 * 1024),
        **options,
    )


def in_hbm(array):
    return pltpu.with_memory_space_constraint(array, pltpu.HBM)


def cut_body(upstream, grads, near, far, pieces, sems):
    cap = near.shape[0]
    count, _, width = pieces.shape
    copies = [
        pltpu.make_async_copy(upstream.at[pl.ds(cap, cap), :], near, sems.at[0]),
        pltpu.make_async_copy(upstream.at[pl.ds(2 * cap, cap), :], far, sems.at[1]),
    ]
    for s in range(count):
        copies.append(
            pltpu.make_async_copy(
                grads.at[:, pl.ds(s * width, width)], pieces.at[s], sems.at[2 + s]
            )
        )
    for copy in copies:
        copy.start()
    for copy in copies:
        copy.wait()


def scale_body(counts, gates, hidden, own, near, far, scales, counts_s, gates_v, hidden_v, sems):
    cap = own.shape[0]
    loads = [
        pltpu.make_async_copy(source, target, sems.at[index])
        for index, (source, target) in enumerate(
            ((counts, counts_s), (gates, gates_v), (hidden, hidden_v))
        )
    ]
    for load in loads:
        load.start()
    for load in loads:
        load.wait()
    rows = lax.broadcasted_iota(jnp.int32, (cap, cap), 0)
    cols = lax.broadcasted_iota(jnp.int32, (cap, cap), 1)
    for b, out in enumerate((own, near, far)):
        gate = gates_v[0:1, b * cap : (b + 1) * cap]
        chosen = jnp.where((rows == cols) & (rows < counts_s[0, b]), gate, 0.0)
        scale = jnp.sum(chosen, axis=1, keepdims=True)
        span = slice(b * cap, (b + 1) * cap)
        out[...] = (scale * hidden_v[span, :].astype(jnp.float32)).astype(jnp.bfloat16)
        scales[span, :] = jnp.broadcast_to(scale, (cap, 128))


def probs_body(latent, key_weight, queries, probs, latent_v, weight_v, query_v, keys, tiles, sems, out_sems):
    seq_len = latent.shape[0]
    count = seq_len // TILE
    loads = [
        pltpu.make_async_copy(key_weight, weight_v, sems.at[0]),
        pltpu.make_async_copy(queries, query_v, sems.at[1]),
    ]
    for tile in range(count):
        span = pl.ds(tile * TILE, TILE)
        loads.append(
            pltpu.make_async_copy(latent.at[span, :], latent_v.at[span, :], sems.at[2 + tile])
        )
    for index in (0, 2, 1, *range(3, 2 + count)):
        loads[index].start()
    factor = math.log2(math.e) / math.sqrt(HEAD_DIM)
    later = lax.broadcasted_iota(jnp.int32, (TILE, TILE), 0) > lax.broadcasted_iota(
        jnp.int32, (TILE, TILE), 1
    )
    stores = []
    loads[0].wait()
    for tile in range(count):
        start, stop = tile * TILE, (tile + 1) * TILE
        loads[2 + tile].wait()
        keys[start:stop, :] = jnp.dot(
            latent_v[start:stop, :], weight_v[...], preferred_element_type=jnp.float32
        ).astype(jnp.bfloat16)
        if tile == 0:
            loads[1].wait()
        for head in range(queries.shape[1] // HEAD_DIM):
            feats = slice(head * HEAD_DIM, (head + 1) * HEAD_DIM)
            query = query_v[start:stop, feats]
            diagonal = lax.dot_general(
                keys[start:stop, feats], query, NT, preferred_element_type=jnp.float32
            )
            diagonal = jnp.where(later, -jnp.inf, diagonal)
            top = jnp.max(diagonal, axis=0, keepdims=True)
            if tile:
                before = lax.dot_general(
                    keys[:start, feats], query, NT, preferred_element_type=jnp.float32
                )
                top = jnp.maximum(top, jnp.max(before, axis=0, keepdims=True))
                before = jnp.exp2((before - top) * factor)
            diagonal = jnp.exp2((diagonal - top) * factor)
            total = jnp.sum(diagonal, axis=0, keepdims=True)
            if tile:
                total = total + jnp.sum(before, axis=0, keepdims=True)
            inverse = 1.0 / total
            tiles[head, start:stop, start:stop] = (diagonal * inverse).astype(jnp.bfloat16)
            if tile:
                tiles[head, :start, start:stop] = (before * inverse).astype(jnp.bfloat16)
            area = (head, pl.ds(0, stop), pl.ds(start, TILE))
            stores.append(
                pltpu.make_async_copy(
                    tiles.at[area], probs.at[area], out_sems.at[head * count + tile]
                )
            )
            stores[-1].start()
    for store in stores:
        store.wait()


def value_body(probs, grads, out, tiles, sems):
    seq_len = grads.shape[0]
    count = seq_len // TILE
    heads = grads.shape[1] // HEAD_DIM
    loads = []
    for head in range(heads):
        for tile in range(count):
            area = (head, pl.ds(0, (tile + 1) * TILE), pl.ds(tile * TILE, TILE))
            loads.append(
                pltpu.make_async_copy(probs.at[area], tiles.at[area], sems.at[head * count + tile])
            )
    for load in loads:
        load.start()
    for head in range(heads):
        feats = slice(head * HEAD_DIM, (head + 1) * HEAD_DIM)
        for tile in range(count):
            loads[head * count + tile].wait()
        for tile in range(count):
            start, stop = tile * TILE, (tile + 1) * TILE
            out[start:stop, feats] = jnp.dot(
                tiles[head, start:stop, start:],
                grads[start:, feats],
                preferred_element_type=jnp.float32,
            ).astype(jnp.bfloat16)


def partial_body(weight, upstream, near, far, own_out, near_out, far_out):
    cap = near.shape[0]
    matrix = weight[...]
    for rows, out in ((near[...], near_out), (far[...], far_out), (upstream[:cap, :], own_out)):
        out[...] = lax.dot_general(
            rows, matrix, NT, preferred_element_type=jnp.float32
        ).astype(jnp.bfloat16)


def weight_body(upstream, own, near_rows, near, far_rows, far, out):
    cap, hid = own.shape
    chunk = 128
    for start in range(0, hid, chunk):
        feats = slice(start, start + chunk)
        total = None
        for left, right in (
            (own[:, feats], upstream[:cap, :]),
            (near[:, feats], near_rows[...]),
            (far[:, feats], far_rows[...]),
        ):
            term = lax.dot_general(left, right, TN, preferred_element_type=jnp.float32)
            term = term.astype(jnp.bfloat16).astype(jnp.float32)
            total = term if total is None else total + term
        out[feats, :] = total.astype(jnp.bfloat16)


def shifted(block, axis, distance):
    devices = range(lax.axis_size(axis))
    route = [(i, (i + distance) % len(devices)) for i in devices]
    return lax.ppermute(block, axis, route)


def on_device(
    queries,
    latent_rows,
    key_weight,
    output_grad,
    down_weight,
    hidden_rows,
    upstream_rows,
    row_gates,
    row_counts,
):
    n_seq = lax.axis_size("seq")
    n_exp = lax.axis_size("exp")
    step = n_exp // 3
    rows, hid = hidden_rows.shape
    cap = rows // 3
    own_rows = rows // n_seq
    wide = upstream_rows.shape[1]
    seq_len, width = queries.shape[1], queries.shape[3]
    tokens = output_grad.shape[1]
    bf16, f32 = jnp.bfloat16, jnp.float32

    def shape(*dims, kind=bf16):
        return jax.ShapeDtypeStruct(dims, kind)

    up_near, up_far, pieces = call(
        cut_body,
        [shape(cap, wide), shape(cap, wide), shape(n_seq, tokens, width)],
        [HBM, HBM],
        outs=HBM,
        scratch_shapes=[pltpu.SemaphoreType.DMA((2 + n_seq,))],
        name="cut",
    )(in_hbm(upstream_rows), in_hbm(output_grad.reshape(tokens, n_seq * width)))
    up_near = shifted(up_near, "exp", -step)
    up_far = shifted(up_far, "exp", -2 * step)
    head_grads = lax.all_to_all(pieces, "seq", split_axis=0, concat_axis=0, tiled=True)

    own, near, far, scales = call(
        scale_body,
        [shape(cap, hid)] * 3 + [shape(rows, 128, kind=f32)],
        [HBM, HBM, HBM],
        scratch_shapes=[
            pltpu.SMEM((1, 3), jnp.int32),
            pltpu.VMEM((1, rows), f32),
            pltpu.VMEM((rows, hid), bf16),
            pltpu.SemaphoreType.DMA((3,)),
        ],
        name="scale",
    )(in_hbm(row_counts), in_hbm(row_gates.reshape(1, rows)), in_hbm(hidden_rows))
    near = shifted(near, "exp", -step)
    far = shifted(far, "exp", -2 * step)

    heads = width // HEAD_DIM
    count = seq_len // TILE
    probs = call(
        probs_body,
        pltpu.HBM((heads, seq_len, seq_len), bf16),
        [HBM, HBM, HBM],
        outs=HBM,
        scratch_shapes=[
            pltpu.VMEM(latent_rows.shape[1:], bf16),
            pltpu.VMEM((key_weight.shape[0], width), bf16),
            pltpu.VMEM((seq_len, width), bf16),
            pltpu.VMEM((seq_len, width), bf16),
            pltpu.VMEM((heads, seq_len, seq_len), bf16),
            pltpu.SemaphoreType.DMA((2 + count,)),
            pltpu.SemaphoreType.DMA((heads * count,)),
        ],
        limit=20,
        name="probs",
    )(
        in_hbm(latent_rows[0]),
        in_hbm(key_weight.reshape(key_weight.shape[0], width)),
        in_hbm(queries.reshape(seq_len, width)),
    )
    up_near, up_far, probs = lax.optimization_barrier((up_near, up_far, probs))

    part_own, part_near, part_far = call(
        partial_body, [shape(cap, hid)] * 3, [VMEM] * 4, name="parts"
    )(down_weight[0], upstream_rows, up_near, up_far)
    part_near = shifted(part_near, "exp", step)
    part_far = shifted(part_far, "exp", 2 * step)
    parts = jnp.concatenate([part_own, part_near, part_far], axis=0)
    shares = lax.all_to_all(
        parts.reshape(n_seq, own_rows, hid), "seq", split_axis=0, concat_axis=0, tiled=True
    )
    weight_grad = call(weight_body, shape(hid, wide), [VMEM] * 6, name="weight")(
        upstream_rows, own, up_near, near, up_far, far
    )[None]
    value_grad = call(
        value_body,
        shape(seq_len, width),
        [HBM, VMEM],
        scratch_shapes=[
            pltpu.VMEM((heads, seq_len, seq_len), bf16),
            pltpu.SemaphoreType.DMA((heads * count,)),
        ],
        name="value",
    )(in_hbm(probs), head_grads.reshape(seq_len, width)).reshape(queries.shape)

    row_start = lax.axis_index("seq") * own_rows
    own_scale = lax.dynamic_slice(scales, (row_start, 0), (own_rows, 1))
    hidden_grad = jnp.sum(shares.astype(f32), axis=0) * own_scale
    return (value_grad, hidden_grad, weight_grad)


def solution(mesh):
    placed = (
        P("exp", None, "dp", "seq"),
        P("exp", None, None),
        P(None, "dp", "seq"),
        P("exp", "seq", "dp", None),
        P("exp", "dp", "seq"),
        P("exp", "dp"),
        P("exp", "seq"),
        P("exp"),
        P("exp", None),
    )
    return jax.shard_map(
        on_device,
        mesh=mesh,
        in_specs=placed,
        out_specs=(P("exp", None, "dp", "seq"), P(("exp", "seq"), "dp"), P("exp", "dp", "seq")),
        check_vma=False,
    )
```

time: 82.4 us -> 111 us (1.35)
  the two profiles are of different devices: /device:TPU:4 before, /device:TPU:2 now
where the time goes in v2:
time: 111 us
  starting transfers between devices  42 us (38%)
  Pallas kernels  29.8 us (27%)
  waiting for transfers between devices  22 us (20%)
  blocking collectives  15.4 us (14%)
    ppermute x6, starting transfers between devices, shifted(): return lax.ppermute(block, axis, route)  37.1 us
    ppermute x6, waiting for transfers between devices, shifted(): return lax.ppermute(block, axis, route)  22 us
    pallas_call x1, Pallas kernels, on_device(): call(cut_body, [shape(cap, wide), shape(cap, wide), shape(n_seq, tokens,...  17.1 us
    all_to_all x1, blocking collectives, on_device(): lax.all_to_all(parts.reshape(n_seq, own_rows, hid), 'seq', split_axis=0,...  15.4 us
    pallas_call x1, Pallas kernels, on_device(): call(probs_body, pltpu.HBM((heads, seq_len, seq_len), bf16), [HBM, HBM, H...  5.6 us
    all_to_all x1, starting transfers between devices, on_device(): lax.all_to_all(pieces, 'seq', split_axis=0, concat_axis=0, tiled=True)  4.86 us
    pallas_call x1, Pallas kernels, on_device(): call(value_body, shape(seq_len, width), [HBM, VMEM], scratch_shapes=[pltp...  3.17 us
  transfers between devices with their start and end apart: 7, of which 5 were waited for; matrix products, arithmetic and copies ran while one was open for 1% of the time, Pallas kernels for 8%

profile of v2, /device:TPU:2, one launch (start us, length us, event | category | flops | bytes accessed | tf_op | source)
XLA Modules:
  0.0 110.8 jit_solution(9314705294977574587)
XLA Ops:
  0.6 0.0 copy-start
  0.6 0.0 copy-start.1
  0.7 17.1 %cut.1 = (bf16[64,896]{1,0:T(8,128)(2,1)S(1)}, bf16[64,896]{1,0:T(8,128)(2,1)S(1)}, bf16[8,128,256]{2,1,0:T(8,128)(2,1)}) custom-call(bf16[192,896]{1,0:T(8,128)(2,1)} %upstream.5, bf16[128,2048]{1,0:T(8,128)(2,1)} %bitcast.17), custom_call_target="tpu_custom_call" | custom-call | tf_op jit(solution)/shard_map/cut/pallas_call | solution.py:221
  17.7 19.6 %collective-permute-start = (bf16[64,896]{1,0:T(8,128)(2,1)S(1)}, bf16[64,896]{1,0:T(8,128)(2,1)S(1)}, u32[]{:S(2)}, u32[]{:S(2)}) collective-permute-start(bf16[64,896]{1,0:T(8,128)(2,1)S(1)} %get-tuple-element.16), channel_id=1, source_target_pairs={{0,704},{32,736},{64,768},{96,800},{128,832},{160,864},{192,896},{... | collective-permute-start | bytes 344072 | tf_op jit(solution)/shard_map/ppermute | solution.py:193
  37.3 1.9 %collective-permute-start.1 = (bf16[64,896]{1,0:T(8,128)(2,1)S(1)}, bf16[64,896]{1,0:T(8,128)(2,1)S(1)}, u32[]{:S(2)}, u32[]{:S(2)}) collective-permute-start(bf16[64,896]{1,0:T(8,128)(2,1)S(1)} %get-tuple-element.17), channel_id=1, source_target_pairs={{0,384},{32,416},{64,448},{96,480},{128,512},{160,544},{192,576},{... | collective-permute-start | bytes 344072 | tf_op jit(solution)/shard_map/ppermute | solution.py:193
  39.3 5.6 %probs.1 = bf16[2,1024,1024]{2,1,0:T(8,128)(2,1)} custom-call(bf16[1024,512]{1,0:T(8,128)(2,1)} %bitcast.12, bf16[512,256]{1,0:T(8,128)(2,1)} %bitcast.18, bf16[1024,256]{1,0:T(8,128)(2,1)} %bitcast.15), custom_call_target="tpu_custom_call" | custom-call | tf_op jit(solution)/shard_map/probs/pallas_call | solution.py:250
  44.9 0.0 collective-permute-done.near.near_rows
  44.9 6.4 %collective-permute-done.1.far.far_rows = bf16[64,896]{1,0:T(8,128)(2,1)S(1)} collective-permute-done((bf16[64,896]{1,0:T(8,128)(2,1)S(1)}, bf16[64,896]{1,0:T(8,128)(2,1)S(1)}, u32[]{:S(2)}, u32[]{:S(2)}) %collective-permute-start.1) | collective-permute-done | bytes 114720 | tf_op jit(solution)/shard_map/ppermute | solution.py:193
  51.3 0.0 copy-done
  51.3 0.0 copy-done.1
  51.3 1.0 parts.1
  52.2 3.0 %collective-permute-start.3 = (bf16[64,512]{1,0:T(8,128)(2,1)S(1)}, bf16[64,512]{1,0:T(8,128)(2,1)S(1)}, u32[]{:S(2)}, u32[]{:S(2)}) collective-permute-start(bf16[64,512]{1,0:T(8,128)(2,1)S(1)} %get-tuple-element.24), channel_id=1, source_target_pairs={{0,640},{32,672},{64,704},{96,736},{128,768},{160,800},{192,832},{... | collective-permute-start | bytes 196616 | tf_op jit(solution)/shard_map/ppermute | solution.py:193
  55.2 3.3 %collective-permute-start.2 = (bf16[64,512]{1,0:T(8,128)(2,1)S(1)}, bf16[64,512]{1,0:T(8,128)(2,1)S(1)}, u32[]{:S(2)}, u32[]{:S(2)}) collective-permute-start(bf16[64,512]{1,0:T(8,128)(2,1)S(1)} %get-tuple-element.23), channel_id=1, source_target_pairs={{0,320},{32,352},{64,384},{96,416},{128,448},{160,480},{192,512},{... | collective-permute-start | bytes 196616 | tf_op jit(solution)/shard_map/ppermute | solution.py:193
  58.5 3.2 %collective-permute-done.3 = bf16[64,512]{1,0:T(8,128)(2,1)S(1)} collective-permute-done((bf16[64,512]{1,0:T(8,128)(2,1)S(1)}, bf16[64,512]{1,0:T(8,128)(2,1)S(1)}, u32[]{:S(2)}, u32[]{:S(2)}) %collective-permute-start.3) | collective-permute-done | bytes 65568 | tf_op jit(solution)/shard_map/ppermute | solution.py:193
  61.7 8.2 %collective-permute-done.2 = bf16[64,512]{1,0:T(8,128)(2,1)S(1)} collective-permute-done((bf16[64,512]{1,0:T(8,128)(2,1)S(1)}, bf16[64,512]{1,0:T(8,128)(2,1)S(1)}, u32[]{:S(2)}, u32[]{:S(2)}) %collective-permute-start.2) | collective-permute-done | bytes 65568 | tf_op jit(solution)/shard_map/ppermute | solution.py:193
  69.9 15.4 %all_to_all.10 = bf16[8,24,512]{2,1,0:T(8,128)(2,1)S(1)} all-to-all(bf16[8,24,512]{2,1,0:T(8,128)(2,1)S(1)} %bitcast.14), channel_id=1, replica_groups=mesh['exp'=32,'seq'=8,'dp'=4] {'seq'}, dimensions={0} | all-to-all | bytes 393216 | tf_op jit(solution)/shard_map/all_to_all | solution.py:279
  85.3 4.9 %all-to-all-start = ((bf16[8,128,256]{2,1,0:T(8,128)(2,1)}), bf16[8,128,256]{2,1,0:T(8,128)(2,1)S(1)}, u32[]{:S(2)}, u32[]{:S(2)}) async-start(bf16[8,128,256]{2,1,0:T(8,128)(2,1)} %get-tuple-element.19), calls=%async_computation | async-start | bytes 1048576 | tf_op jit(solution)/shard_map/all_to_all | solution.py:231
  90.1 1.1 %scale.1 = (bf16[64,512]{1,0:T(8,128)(2,1)S(1)}, bf16[64,512]{1,0:T(8,128)(2,1)S(1)}, bf16[64,512]{1,0:T(8,128)(2,1)S(1)}, f32[192,128]{1,0:T(8,128)S(1)}) custom-call(s32[1,3]{1,0:T(1,128)} %counts.1, f32[1,192]{1,0:T(1,128)} %bitcast.19, bf16[192,512]{1,0:T(8,128)(2,1)} %hidden.1), custom_call_target="tpu_custom_call" | custom-call | tf_op jit(solution)/shard_map/scale/pallas_call | solution.py:233
  91.3 4.5 %collective-permute-start.4 = (bf16[64,512]{1,0:T(8,128)(2,1)S(1)}, bf16[64,512]{1,0:T(8,128)(2,1)S(1)}, u32[]{:S(2)}, u32[]{:S(2)}) collective-permute-start(bf16[64,512]{1,0:T(8,128)(2,1)S(1)} %get-tuple-element.27), channel_id=1, source_target_pairs={{0,704},{32,736},{64,768},{96,800},{128,832},{160,864},{192,896},{... | collective-permute-start | bytes 196616 | tf_op jit(solution)/shard_map/ppermute | solution.py:193
  95.8 4.8 %collective-permute-start.5 = (bf16[64,512]{1,0:T(8,128)(2,1)S(1)}, bf16[64,512]{1,0:T(8,128)(2,1)S(1)}, u32[]{:S(2)}, u32[]{:S(2)}) collective-permute-start(bf16[64,512]{1,0:T(8,128)(2,1)S(1)} %get-tuple-element.28), channel_id=1, source_target_pairs={{0,384},{32,416},{64,448},{96,480},{128,512},{160,544},{192,576},{... | collective-permute-start | bytes 196616 | tf_op jit(solution)/shard_map/ppermute | solution.py:193
  100.7 0.1 dynamic-slice_reduce_fusion
  100.8 3.0 %collective-permute-done.4.near = bf16[64,512]{1,0:T(8,128)(2,1)S(1)} collective-permute-done((bf16[64,512]{1,0:T(8,128)(2,1)S(1)}, bf16[64,512]{1,0:T(8,128)(2,1)S(1)}, u32[]{:S(2)}, u32[]{:S(2)}) %collective-permute-start.4) | collective-permute-done | bytes 65568 | tf_op jit(solution)/shard_map/ppermute | solution.py:193
  103.8 1.3 %collective-permute-done.5.far = bf16[64,512]{1,0:T(8,128)(2,1)S(1)} collective-permute-done((bf16[64,512]{1,0:T(8,128)(2,1)S(1)}, bf16[64,512]{1,0:T(8,128)(2,1)S(1)}, u32[]{:S(2)}, u32[]{:S(2)}) %collective-permute-start.5) | collective-permute-done | bytes 65568 | tf_op jit(solution)/shard_map/ppermute | solution.py:193
  105.0 1.8 %weight.1 = bf16[512,896]{1,0:T(8,128)(2,1)} custom-call(bf16[192,896]{1,0:T(8,128)(2,1)S(1)} %copy-done, bf16[64,512]{1,0:T(8,128)(2,1)S(1)} %get-tuple-element.26.own, bf16[64,896]{1,0:T(8,128)(2,1)S(1)} %collective-permute-done.near.near_rows, bf16[64,512]{1,0:T(8,128)(2,1)S(1)} %collective-permute-done.4.near, ...), custom_call_target="tpu_custom_call" | custom-call | tf_op jit(solution)/shard_map/weight/pallas_call | solution.py:282
  106.9 0.7 broadcast_multiply_fusion
  107.6 0.0 all-to-all-done
  107.6 3.2 %value.1 = bf16[1024,256]{1,0:T(8,128)(2,1)} custom-call(bf16[2,1024,1024]{2,1,0:T(8,128)(2,1)} %probs.1, bf16[1024,256]{1,0:T(8,128)(2,1)S(1)} %bitcast.10), custom_call_target="tpu_custom_call" | custom-call | tf_op jit(solution)/shard_map/value/pallas_call | solution.py:285
  (2 shorter events, 0.0 us)
Async XLA Ops:
  0.6 50.6 %copy-start = (bf16[192,896]{1,0:T(8,128)(2,1)S(1)}, bf16[192,896]{1,0:T(8,128)(2,1)}, u32[]{:S(2)}) copy-start(bf16[192,896]{1,0:T(8,128)(2,1)} %upstream.5) | copy-start | bytes 1032196
  0.6 50.6 %copy-start.1 = (bf16[1,512,896]{2,1,0:T(8,128)(2,1)S(1)}, bf16[1,512,896]{2,1,0:T(8,128)(2,1)}, u32[]{:S(2)}) copy-start(bf16[1,512,896]{2,1,0:T(8,128)(2,1)} %param.13) | copy-start | bytes 2752516
  17.7 27.1 %collective-permute-start = (bf16[64,896]{1,0:T(8,128)(2,1)S(1)}, bf16[64,896]{1,0:T(8,128)(2,1)S(1)}, u32[]{:S(2)}, u32[]{:S(2)}) collective-permute-start(bf16[64,896]{1,0:T(8,128)(2,1)S(1)} %get-tuple-element.16), channel_id=1, source_target_pairs={{0,704},{32,736},{64,768},{96,800},{128,832},{160,864},{192,896},{... | collective-permute-start | bytes 344072 | tf_op jit(solution)/shard_map/ppermute | solution.py:193
  37.3 13.9 %collective-permute-start.1 = (bf16[64,896]{1,0:T(8,128)(2,1)S(1)}, bf16[64,896]{1,0:T(8,128)(2,1)S(1)}, u32[]{:S(2)}, u32[]{:S(2)}) collective-permute-start(bf16[64,896]{1,0:T(8,128)(2,1)S(1)} %get-tuple-element.17), channel_id=1, source_target_pairs={{0,384},{32,416},{64,448},{96,480},{128,512},{160,544},{192,576},{... | collective-permute-start | bytes 344072 | tf_op jit(solution)/shard_map/ppermute | solution.py:193
  52.2 9.4 %collective-permute-start.3 = (bf16[64,512]{1,0:T(8,128)(2,1)S(1)}, bf16[64,512]{1,0:T(8,128)(2,1)S(1)}, u32[]{:S(2)}, u32[]{:S(2)}) collective-permute-start(bf16[64,512]{1,0:T(8,128)(2,1)S(1)} %get-tuple-element.24), channel_id=1, source_target_pairs={{0,640},{32,672},{64,704},{96,736},{128,768},{160,800},{192,832},{... | collective-permute-start | bytes 196616 | tf_op jit(solution)/shard_map/ppermute | solution.py:193
  55.2 14.6 %collective-permute-start.2 = (bf16[64,512]{1,0:T(8,128)(2,1)S(1)}, bf16[64,512]{1,0:T(8,128)(2,1)S(1)}, u32[]{:S(2)}, u32[]{:S(2)}) collective-permute-start(bf16[64,512]{1,0:T(8,128)(2,1)S(1)} %get-tuple-element.23), channel_id=1, source_target_pairs={{0,320},{32,352},{64,384},{96,416},{128,448},{160,480},{192,512},{... | collective-permute-start | bytes 196616 | tf_op jit(solution)/shard_map/ppermute | solution.py:193
  85.3 22.3 %all-to-all-start = ((bf16[8,128,256]{2,1,0:T(8,128)(2,1)}), bf16[8,128,256]{2,1,0:T(8,128)(2,1)S(1)}, u32[]{:S(2)}, u32[]{:S(2)}) async-start(bf16[8,128,256]{2,1,0:T(8,128)(2,1)} %get-tuple-element.19), calls=%async_computation | async-start | bytes 1048576 | tf_op jit(solution)/shard_map/all_to_all | solution.py:231
  91.3 12.5 %collective-permute-start.4 = (bf16[64,512]{1,0:T(8,128)(2,1)S(1)}, bf16[64,512]{1,0:T(8,128)(2,1)S(1)}, u32[]{:S(2)}, u32[]{:S(2)}) collective-permute-start(bf16[64,512]{1,0:T(8,128)(2,1)S(1)} %get-tuple-element.27), channel_id=1, source_target_pairs={{0,704},{32,736},{64,768},{96,800},{128,832},{160,864},{192,896},{... | collective-permute-start | bytes 196616 | tf_op jit(solution)/shard_map/ppermute | solution.py:193
  95.8 9.2 %collective-permute-start.5 = (bf16[64,512]{1,0:T(8,128)(2,1)S(1)}, bf16[64,512]{1,0:T(8,128)(2,1)S(1)}, u32[]{:S(2)}, u32[]{:S(2)}) collective-permute-start(bf16[64,512]{1,0:T(8,128)(2,1)S(1)} %get-tuple-element.28), channel_id=1, source_target_pairs={{0,384},{32,416},{64,448},{96,480},{128,512},{160,544},{192,576},{... | collective-permute-start | bytes 196616 | tf_op jit(solution)/shard_map/ppermute | solution.py:193

commit v3 on v2

--- a/solution.py
+++ b/solution.py
@@ -10,6 +10,7 @@
 
 HEAD_DIM = 128
 TILE = 256
+CUTS = ((0, 96), (96, 32))
 NT = (((1,), (1,)), ((), ()))
 TN = (((0,), (0,)), ((), ()))
 VMEM = pl.BlockSpec(memory_space=pltpu.VMEM)
@@ -32,32 +33,21 @@
     return pltpu.with_memory_space_constraint(array, pltpu.HBM)
 
 
-def cut_body(upstream, grads, near, far, pieces, sems):
-    cap = near.shape[0]
-    count, _, width = pieces.shape
-    copies = [
-        pltpu.make_async_copy(upstream.at[pl.ds(cap, cap), :], near, sems.at[0]),
-        pltpu.make_async_copy(upstream.at[pl.ds(2 * cap, cap), :], far, sems.at[1]),
-    ]
-    for s in range(count):
-        copies.append(
-            pltpu.make_async_copy(
-                grads.at[:, pl.ds(s * width, width)], pieces.at[s], sems.at[2 + s]
-            )
-        )
-    for copy in copies:
-        copy.start()
-    for copy in copies:
-        copy.wait()
-
-
-def scale_body(counts, gates, hidden, own, near, far, scales, counts_s, gates_v, hidden_v, sems):
+def pack_body(
+    counts, gates, hidden, upstream, near, far, own, scales, counts_s, gates_v, hidden_v, sems
+):
     cap = own.shape[0]
+    wide = upstream.shape[1]
+    sources = (
+        (counts, counts_s),
+        (gates, gates_v),
+        (hidden, hidden_v),
+        (upstream.at[pl.ds(cap, cap), :], near.at[:, pl.ds(0, wide)]),
+        (upstream.at[pl.ds(2 * cap, cap), :], far.at[:, pl.ds(0, wide)]),
+    )
     loads = [
         pltpu.make_async_copy(source, target, sems.at[index])
-        for index, (source, target) in enumerate(
-            ((counts, counts_s), (gates, gates_v), (hidden, hidden_v))
-        )
+        for index, (source, target) in enumerate(sources)
     ]
     for load in loads:
         load.start()
@@ -70,8 +60,40 @@
         chosen = jnp.where((rows == cols) & (rows < counts_s[0, b]), gate, 0.0)
         scale = jnp.sum(chosen, axis=1, keepdims=True)
         span = slice(b * cap, (b + 1) * cap)
-        out[...] = (scale * hidden_v[span, :].astype(jnp.float32)).astype(jnp.bfloat16)
+        scaled = (scale * hidden_v[span, :].astype(jnp.float32)).astype(jnp.bfloat16)
+        if b:
+            out[:, wide:] = scaled
+        else:
+            out[...] = scaled
         scales[span, :] = jnp.broadcast_to(scale, (cap, 128))
+
+
+def split_body(grads, *refs):
+    pieces, (pieces_v, load_sems, store_sems) = refs[: len(CUTS)], refs[len(CUTS) :]
+    count, _, width = pieces_v.shape
+    loads = [
+        pltpu.make_async_copy(
+            grads.at[:, pl.ds(s * width, width)], pieces_v.at[s], load_sems.at[s]
+        )
+        for s in range(count)
+    ]
+    stores = [
+        pltpu.make_async_copy(
+            pieces_v.at[s, pl.ds(first, size), :],
+            pieces[index].at[s],
+            store_sems.at[s * len(CUTS) + index],
+        )
+        for s in range(count)
+        for index, (first, size) in enumerate(CUTS)
+    ]
+    for load in loads:
+        load.start()
+    for s, load in enumerate(loads):
+        load.wait()
+        for store in stores[s * len(CUTS) : (s + 1) * len(CUTS)]:
+            store.start()
+    for store in stores:
+        store.wait()
 
 
 def probs_body(latent, key_weight, queries, probs, latent_v, weight_v, query_v, keys, tiles, sems, out_sems):
@@ -135,7 +157,9 @@
         store.wait()
 
 
-def value_body(probs, grads, out, tiles, sems):
+def value_body(probs, *refs):
+    n_cuts = len(CUTS)
+    shares, (out, tiles, grads, sems) = refs[:n_cuts], refs[n_cuts:]
     seq_len = grads.shape[0]
     count = seq_len // TILE
     heads = grads.shape[1] // HEAD_DIM
@@ -148,6 +172,10 @@
             )
     for load in loads:
         load.start()
+    tokens = sum(size for _, size in CUTS)
+    for (first, size), share in zip(CUTS, shares):
+        for s in range(share.shape[0]):
+            grads[s * tokens + first : s * tokens + first + size, :] = share[s]
     for head in range(heads):
         feats = slice(head * HEAD_DIM, (head + 1) * HEAD_DIM)
         for tile in range(count):
@@ -161,25 +189,28 @@
             ).astype(jnp.bfloat16)
 
 
-def partial_body(weight, upstream, near, far, own_out, near_out, far_out):
+def partial_body(weight, upstream, near, far, out):
     cap = near.shape[0]
+    wide = weight.shape[1]
     matrix = weight[...]
-    for rows, out in ((near[...], near_out), (far[...], far_out), (upstream[:cap, :], own_out)):
-        out[...] = lax.dot_general(
+    for b, rows in enumerate((upstream[:cap, :], near[:, :wide], far[:, :wide])):
+        out[b * cap : (b + 1) * cap, :] = lax.dot_general(
             rows, matrix, NT, preferred_element_type=jnp.float32
         ).astype(jnp.bfloat16)
 
 
-def weight_body(upstream, own, near_rows, near, far_rows, far, out):
+def weight_body(upstream, own, near, far, out):
     cap, hid = own.shape
+    wide = upstream.shape[1]
     chunk = 128
     for start in range(0, hid, chunk):
         feats = slice(start, start + chunk)
+        packed = slice(wide + start, wide + start + chunk)
         total = None
         for left, right in (
             (own[:, feats], upstream[:cap, :]),
-            (near[:, feats], near_rows[...]),
-            (far[:, feats], far_rows[...]),
+            (near[:, packed], near[:, :wide]),
+            (far[:, packed], far[:, :wide]),
         ):
             term = lax.dot_general(left, right, TN, preferred_element_type=jnp.float32)
             term = term.astype(jnp.bfloat16).astype(jnp.float32)
@@ -218,32 +249,42 @@
     def shape(*dims, kind=bf16):
         return jax.ShapeDtypeStruct(dims, kind)
 
-    up_near, up_far, pieces = call(
-        cut_body,
-        [shape(cap, wide), shape(cap, wide), shape(n_seq, tokens, width)],
-        [HBM, HBM],
-        outs=HBM,
-        scratch_shapes=[pltpu.SemaphoreType.DMA((2 + n_seq,))],
-        name="cut",
-    )(in_hbm(upstream_rows), in_hbm(output_grad.reshape(tokens, n_seq * width)))
-    up_near = shifted(up_near, "exp", -step)
-    up_far = shifted(up_far, "exp", -2 * step)
-    head_grads = lax.all_to_all(pieces, "seq", split_axis=0, concat_axis=0, tiled=True)
-
-    own, near, far, scales = call(
-        scale_body,
-        [shape(cap, hid)] * 3 + [shape(rows, 128, kind=f32)],
-        [HBM, HBM, HBM],
+    near, far, own, scales = call(
+        pack_body,
+        [shape(cap, wide + hid)] * 2 + [shape(cap, hid), shape(rows, 128, kind=f32)],
+        [HBM] * 4,
         scratch_shapes=[
             pltpu.SMEM((1, 3), jnp.int32),
             pltpu.VMEM((1, rows), f32),
             pltpu.VMEM((rows, hid), bf16),
-            pltpu.SemaphoreType.DMA((3,)),
+            pltpu.SemaphoreType.DMA((5,)),
         ],
-        name="scale",
-    )(in_hbm(row_counts), in_hbm(row_gates.reshape(1, rows)), in_hbm(hidden_rows))
+        name="pack",
+    )(
+        in_hbm(row_counts),
+        in_hbm(row_gates.reshape(1, rows)),
+        in_hbm(hidden_rows),
+        in_hbm(upstream_rows),
+    )
     near = shifted(near, "exp", -step)
     far = shifted(far, "exp", -2 * step)
+    pieces = call(
+        split_body,
+        [pltpu.HBM((n_seq, size, width), bf16) for _, size in CUTS],
+        [HBM],
+        outs=HBM,
+        scratch_shapes=[
+            pltpu.VMEM((n_seq, tokens, width), bf16),
+            pltpu.SemaphoreType.DMA((n_seq,)),
+            pltpu.SemaphoreType.DMA((n_seq * len(CUTS),)),
+        ],
+        name="split",
+    )(in_hbm(output_grad.reshape(tokens, n_seq * width)))
+    head_grads = []
+    for piece in pieces:
+        head_grads.append(
+            lax.all_to_all(piece, "seq", split_axis=0, concat_axis=0, tiled=True)
+        )
 
     heads = width // HEAD_DIM
     count = seq_len // TILE
@@ -268,34 +309,49 @@
         in_hbm(key_weight.reshape(key_weight.shape[0], width)),
         in_hbm(queries.reshape(seq_len, width)),
     )
-    up_near, up_far, probs = lax.optimization_barrier((up_near, up_far, probs))
-
-    part_own, part_near, part_far = call(
-        partial_body, [shape(cap, hid)] * 3, [VMEM] * 4, name="parts"
-    )(down_weight[0], upstream_rows, up_near, up_far)
-    part_near = shifted(part_near, "exp", step)
-    part_far = shifted(part_far, "exp", 2 * step)
-    parts = jnp.concatenate([part_own, part_near, part_far], axis=0)
+    near, far, probs = lax.optimization_barrier((near, far, probs))
+
+    parts = call(partial_body, shape(rows, hid), [VMEM] * 4, name="parts")(
+        down_weight[0], upstream_rows, near, far
+    )
     shares = lax.all_to_all(
         parts.reshape(n_seq, own_rows, hid), "seq", split_axis=0, concat_axis=0, tiled=True
     )
-    weight_grad = call(weight_body, shape(hid, wide), [VMEM] * 6, name="weight")(
-        upstream_rows, own, up_near, near, up_far, far
+    weight_grad = call(weight_body, shape(hid, wide), [VMEM] * 4, name="weight")(
+        upstream_rows, own, near, far
     )[None]
     value_grad = call(
         value_body,
         shape(seq_len, width),
-        [HBM, VMEM],
+        [HBM] + [VMEM] * len(CUTS),
         scratch_shapes=[
             pltpu.VMEM((heads, seq_len, seq_len), bf16),
+            pltpu.VMEM((seq_len, width), bf16),
             pltpu.SemaphoreType.DMA((heads * count,)),
         ],
         name="value",
-    )(in_hbm(probs), head_grads.reshape(seq_len, width)).reshape(queries.shape)
-
+    )(in_hbm(probs), *head_grads).reshape(queries.shape)
+
+    summed = jnp.sum(shares.astype(f32), axis=0)
+    needs = [
+        [b for b in (1, 2) if s * own_rows < (b + 1) * cap and (s + 1) * own_rows > b * cap]
+        for s in range(n_seq)
+    ]
+    backs = []
+    for turn in range(2):
+        route = [
+            (e * n_seq + s, (e + blocks[turn] * step) % n_exp * n_seq + s)
+            for s, blocks in enumerate(needs)
+            if turn < len(blocks)
+            for e in range(n_exp)
+        ]
+        backs.append(lax.ppermute(summed.astype(bf16), ("exp", "seq"), route).astype(f32))
     row_start = lax.axis_index("seq") * own_rows
+    block_ids = ((row_start + jnp.arange(own_rows)) // cap)[:, None]
+    second_of_two = (block_ids == 2) & (row_start // cap == 1)
+    total = jnp.where(block_ids == 0, summed, jnp.where(second_of_two, backs[1], backs[0]))
     own_scale = lax.dynamic_slice(scales, (row_start, 0), (own_rows, 1))
-    hidden_grad = jnp.sum(shares.astype(f32), axis=0) * own_scale
+    hidden_grad = total * own_scale
     return (value_grad, hidden_grad, weight_grad)
 
 

time: 111 us -> 88.4 us (0.80)
  the two profiles are of different devices: /device:TPU:2 before, /device:TPU:4 now
where the time goes in v3:
time: 88.4 us; the launch traced here: 87.9 us
  starting transfers between devices  38.1 us (43%)
  waiting for transfers between devices  19 us (21%)
  Pallas kernels  14.8 us (17%)
  blocking collectives  14.4 us (16%)
    all_to_all x2, starting transfers between devices, on_device(): lax.all_to_all(piece, 'seq', split_axis=0, concat_axis=0, tiled=True)  23.1 us
    all_to_all x1, blocking collectives, on_device(): lax.all_to_all(parts.reshape(n_seq, own_rows, hid), 'seq', split_axis=0,...  14.4 us
    ppermute x2, starting transfers between devices, shifted(): return lax.ppermute(block, axis, route)  12.4 us
    ppermute x2, waiting for transfers between devices, shifted(): return lax.ppermute(block, axis, route)  10.1 us
    ppermute x2, waiting for transfers between devices, on_device(): lax.ppermute(summed.astype(bf16), ('exp', 'seq'), route).astype(f32)  8.9 us
    pallas_call x1, Pallas kernels, on_device(): call(probs_body, pltpu.HBM((heads, seq_len, seq_len), bf16), [HBM, HBM, H...  5.61 us
    pallas_call x1, Pallas kernels, on_device(): call(value_body, shape(seq_len, width), [HBM] + [VMEM] * len(CUTS), scrat...  3.17 us
    ppermute x2, starting transfers between devices, on_device(): lax.ppermute(summed.astype(bf16), ('exp', 'seq'), route).astype(f32)  2.65 us
  transfers between devices with their start and end apart: 6, of which 3 were waited for; matrix products, arithmetic and copies ran while one was open for 1% of the time, Pallas kernels for 11%

profile of v3, /device:TPU:4, one launch (start us, length us, event | category | flops | bytes accessed | tf_op | source)
XLA Modules:
  0.0 87.9 jit_solution(16185541429515091998)
XLA Ops:
  0.6 0.0 copy-start
  0.6 0.0 copy-start.1
  0.7 2.0 %split.1 = (bf16[8,96,256]{2,1,0:T(8,128)(2,1)}, bf16[8,32,256]{2,1,0:T(8,128)(2,1)}) custom-call(bf16[128,2048]{1,0:T(8,128)(2,1)} %bitcast.15), custom_call_target="tpu_custom_call" | custom-call | tf_op jit(solution)/shard_map/split/pallas_call | solution.py:271
  2.7 16.4 %all-to-all-start.1 = ((bf16[8,32,256]{2,1,0:T(8,128)(2,1)}), bf16[8,32,256]{2,1,0:T(8,128)(2,1)S(1)}, u32[]{:S(2)}, u32[]{:S(2)}) async-start(bf16[8,32,256]{2,1,0:T(8,128)(2,1)} %get-tuple-element.16), calls=%async_computation.1 | async-start | bytes 262144 | tf_op jit(solution)/shard_map/all_to_all | solution.py:286
  19.1 1.3 %pack.1 = (bf16[64,1408]{1,0:T(8,128)(2,1)S(1)}, bf16[64,1408]{1,0:T(8,128)(2,1)S(1)}, bf16[64,512]{1,0:T(8,128)(2,1)S(1)}, f32[192,128]{1,0:T(8,128)S(1)}) custom-call(s32[1,3]{1,0:T(1,128)} %counts.1, f32[1,192]{1,0:T(1,128)} %bitcast.17, bf16[192,512]{1,0:T(8,128)(2,1)} %hidden.1, bf16[192,896]{1,0:T(8,128)(2,1)} %upstream.5), custom_call_target="tpu_custom_call" | custom-call | tf_op jit(solution)/shard_map/pack/pallas_call | solution.py:252
  20.3 10.5 %collective-permute-start = (bf16[64,1408]{1,0:T(8,128)(2,1)S(1)}, bf16[64,1408]{1,0:T(8,128)(2,1)S(1)}, u32[]{:S(2)}, u32[]{:S(2)}) collective-permute-start(bf16[64,1408]{1,0:T(8,128)(2,1)S(1)} %get-tuple-element.12), channel_id=1, source_target_pairs={{0,704},{32,736},{64,768},{96,800},{128,832},{160,864},{192,896},{... | collective-permute-start | bytes 540680 | tf_op jit(solution)/shard_map/ppermute | solution.py:224
  30.8 1.9 %collective-permute-start.1 = (bf16[64,1408]{1,0:T(8,128)(2,1)S(1)}, bf16[64,1408]{1,0:T(8,128)(2,1)S(1)}, u32[]{:S(2)}, u32[]{:S(2)}) collective-permute-start(bf16[64,1408]{1,0:T(8,128)(2,1)S(1)} %get-tuple-element.13), channel_id=1, source_target_pairs={{0,384},{32,416},{64,448},{96,480},{128,512},{160,544},{192,576},{... | collective-permute-start | bytes 540680 | tf_op jit(solution)/shard_map/ppermute | solution.py:224
  32.7 5.6 %probs.1 = bf16[2,1024,1024]{2,1,0:T(8,128)(2,1)} custom-call(bf16[1024,512]{1,0:T(8,128)(2,1)} %bitcast.11, bf16[512,256]{1,0:T(8,128)(2,1)} %bitcast.16, bf16[1024,256]{1,0:T(8,128)(2,1)} %bitcast.13), custom_call_target="tpu_custom_call" | custom-call | tf_op jit(solution)/shard_map/probs/pallas_call | solution.py:291
  38.4 3.4 %collective-permute-done.near = bf16[64,1408]{1,0:T(8,128)(2,1)S(1)} collective-permute-done((bf16[64,1408]{1,0:T(8,128)(2,1)S(1)}, bf16[64,1408]{1,0:T(8,128)(2,1)S(1)}, u32[]{:S(2)}, u32[]{:S(2)}) %collective-permute-start) | collective-permute-done | bytes 180256 | tf_op jit(solution)/shard_map/ppermute | solution.py:224
  41.8 6.6 %collective-permute-done.1.far = bf16[64,1408]{1,0:T(8,128)(2,1)S(1)} collective-permute-done((bf16[64,1408]{1,0:T(8,128)(2,1)S(1)}, bf16[64,1408]{1,0:T(8,128)(2,1)S(1)}, u32[]{:S(2)}, u32[]{:S(2)}) %collective-permute-start.1) | collective-permute-done | bytes 180256 | tf_op jit(solution)/shard_map/ppermute | solution.py:224
  48.4 0.0 copy-done
  48.4 0.0 copy-done.1
  48.4 1.0 %parts.1 = bf16[192,512]{1,0:T(8,128)(2,1)S(1)} custom-call(bf16[512,896]{1,0:T(8,128)(2,1)S(1)} %bitcast.9, bf16[192,896]{1,0:T(8,128)(2,1)S(1)} %copy-done, bf16[64,1408]{1,0:T(8,128)(2,1)S(1)} %collective-permute-done.near, bf16[64,1408]{1,0:T(8,128)(2,1)S(1)} %collective-permute-done.1.far), custom_call_target="tpu_custom_call" | custom-call | tf_op jit(solution)/shard_map/parts/pallas_call | solution.py:314
  49.4 0.0 all-to-all-done.1.refs_1_
  49.4 14.4 %all_to_all.15 = bf16[8,24,512]{2,1,0:T(8,128)(2,1)S(1)} all-to-all(bf16[8,24,512]{2,1,0:T(8,128)(2,1)S(1)} %bitcast.10), channel_id=1, replica_groups=mesh['exp'=32,'seq'=8,'dp'=4] {'seq'}, dimensions={0} | all-to-all | bytes 393216 | tf_op jit(solution)/shard_map/all_to_all | solution.py:317
  63.8 6.7 %all-to-all-start = ((bf16[8,96,256]{2,1,0:T(8,128)(2,1)}), bf16[8,96,256]{2,1,0:T(8,128)(2,1)S(1)}, u32[]{:S(2)}, u32[]{:S(2)}) async-start(bf16[8,96,256]{2,1,0:T(8,128)(2,1)} %get-tuple-element.15), calls=%async_computation | async-start | bytes 786432 | tf_op jit(solution)/shard_map/all_to_all | solution.py:286
  70.5 2.0 %collective-permute-start.3 = (bf16[24,512]{1,0:T(8,128)(2,1)S(1)}, bf16[24,512]{1,0:T(8,128)(2,1)S(1)}, u32[]{:S(2)}, u32[]{:S(2)}) collective-permute-start(bf16[24,512]{1,0:T(8,128)(2,1)S(1)} %convert_element_type.14), channel_id=1, source_target_pairs={{8,328},{40,360},{72,392},{104,424},{136,456},{168,488},{200,520},... | collective-permute-start | bytes 73736 | tf_op jit(solution)/shard_map/ppermute | solution.py:348
  72.5 0.7 collective-permute-start.2
  73.2 0.1 dynamic-slice_reduce_fusion
  73.3 1.8 %weight.1 = bf16[512,896]{1,0:T(8,128)(2,1)} custom-call(bf16[192,896]{1,0:T(8,128)(2,1)S(1)} %copy-done, bf16[64,512]{1,0:T(8,128)(2,1)S(1)} %get-tuple-element.20.own, bf16[64,1408]{1,0:T(8,128)(2,1)S(1)} %collective-permute-done.near, bf16[64,1408]{1,0:T(8,128)(2,1)S(1)} %collective-permute-done.1.far), custom_call_target="tpu_custom_call" | custom-call | tf_op jit(solution)/shard_map/weight/pallas_call | solution.py:320
  75.1 8.9 %collective-permute-done.3 = bf16[24,512]{1,0:T(8,128)(2,1)S(1)} collective-permute-done((bf16[24,512]{1,0:T(8,128)(2,1)S(1)}, bf16[24,512]{1,0:T(8,128)(2,1)S(1)}, u32[]{:S(2)}, u32[]{:S(2)}) %collective-permute-start.3) | collective-permute-done | bytes 24608 | tf_op jit(solution)/shard_map/ppermute | solution.py:348
  84.0 0.0 collective-permute-done.2
  84.0 0.7 select_multiply_fusion
  84.7 0.0 all-to-all-done.refs_0_
  84.7 3.2 %value.1 = bf16[1024,256]{1,0:T(8,128)(2,1)} custom-call(bf16[2,1024,1024]{2,1,0:T(8,128)(2,1)} %probs.1, bf16[8,96,256]{2,1,0:T(8,128)(2,1)S(1)} %all-to-all-done.refs_0_, bf16[8,32,256]{2,1,0:T(8,128)(2,1)S(1)} %all-to-all-done.1.refs_1_), custom_call_target="tpu_custom_call" | custom-call | tf_op jit(solution)/shard_map/value/pallas_call | solution.py:323
  (3 shorter events, 0.1 us)
Async XLA Ops:
  0.6 47.8 %copy-start = (bf16[192,896]{1,0:T(8,128)(2,1)S(1)}, bf16[192,896]{1,0:T(8,128)(2,1)}, u32[]{:S(2)}) copy-start(bf16[192,896]{1,0:T(8,128)(2,1)} %upstream.5) | copy-start | bytes 1032196
  0.6 47.8 %copy-start.1 = (bf16[1,512,896]{2,1,0:T(8,128)(2,1)S(1)}, bf16[1,512,896]{2,1,0:T(8,128)(2,1)}, u32[]{:S(2)}) copy-start(bf16[1,512,896]{2,1,0:T(8,128)(2,1)} %param.13) | copy-start | bytes 2752516
  2.7 46.8 %all-to-all-start.1 = ((bf16[8,32,256]{2,1,0:T(8,128)(2,1)}), bf16[8,32,256]{2,1,0:T(8,128)(2,1)S(1)}, u32[]{:S(2)}, u32[]{:S(2)}) async-start(bf16[8,32,256]{2,1,0:T(8,128)(2,1)} %get-tuple-element.16), calls=%async_computation.1 | async-start | bytes 262144 | tf_op jit(solution)/shard_map/all_to_all | solution.py:286
  20.3 21.4 %collective-permute-start = (bf16[64,1408]{1,0:T(8,128)(2,1)S(1)}, bf16[64,1408]{1,0:T(8,128)(2,1)S(1)}, u32[]{:S(2)}, u32[]{:S(2)}) collective-permute-start(bf16[64,1408]{1,0:T(8,128)(2,1)S(1)} %get-tuple-element.12), channel_id=1, source_target_pairs={{0,704},{32,736},{64,768},{96,800},{128,832},{160,864},{192,896},{... | collective-permute-start | bytes 540680 | tf_op jit(solution)/shard_map/ppermute | solution.py:224
  30.8 17.6 %collective-permute-start.1 = (bf16[64,1408]{1,0:T(8,128)(2,1)S(1)}, bf16[64,1408]{1,0:T(8,128)(2,1)S(1)}, u32[]{:S(2)}, u32[]{:S(2)}) collective-permute-start(bf16[64,1408]{1,0:T(8,128)(2,1)S(1)} %get-tuple-element.13), channel_id=1, source_target_pairs={{0,384},{32,416},{64,448},{96,480},{128,512},{160,544},{192,576},{... | collective-permute-start | bytes 540680 | tf_op jit(solution)/shard_map/ppermute | solution.py:224
  63.8 21.0 %all-to-all-start = ((bf16[8,96,256]{2,1,0:T(8,128)(2,1)}), bf16[8,96,256]{2,1,0:T(8,128)(2,1)S(1)}, u32[]{:S(2)}, u32[]{:S(2)}) async-start(bf16[8,96,256]{2,1,0:T(8,128)(2,1)} %get-tuple-element.15), calls=%async_computation | async-start | bytes 786432 | tf_op jit(solution)/shard_map/all_to_all | solution.py:286
  70.5 13.5 %collective-permute-start.3 = (bf16[24,512]{1,0:T(8,128)(2,1)S(1)}, bf16[24,512]{1,0:T(8,128)(2,1)S(1)}, u32[]{:S(2)}, u32[]{:S(2)}) collective-permute-start(bf16[24,512]{1,0:T(8,128)(2,1)S(1)} %convert_element_type.14), channel_id=1, source_target_pairs={{8,328},{40,360},{72,392},{104,424},{136,456},{168,488},{200,520},... | collective-permute-start | bytes 73736 | tf_op jit(solution)/shard_map/ppermute | solution.py:348
  72.5 11.5 %collective-permute-start.2 = (bf16[24,512]{1,0:T(8,128)(2,1)S(1)}, bf16[24,512]{1,0:T(8,128)(2,1)S(1)}, u32[]{:S(2)}, u32[]{:S(2)}) collective-permute-start(bf16[24,512]{1,0:T(8,128)(2,1)S(1)} %convert_element_type.14), channel_id=1, source_target_pairs={{20,660},{52,692},{84,724},{116,756},{148,788},{180,820},{212,852}... | collective-permute-start | bytes 73736 | tf_op jit(solution)/shard_map/ppermute | solution.py:348

commit v4 on v3

--- a/solution.py
+++ b/solution.py
@@ -10,7 +10,7 @@
 
 HEAD_DIM = 128
 TILE = 256
-CUTS = ((0, 96), (96, 32))
+CUTS = ((0, 128),)
 NT = (((1,), (1,)), ((), ()))
 TN = (((0,), (0,)), ((), ()))
 VMEM = pl.BlockSpec(memory_space=pltpu.VMEM)
@@ -33,11 +33,13 @@
     return pltpu.with_memory_space_constraint(array, pltpu.HBM)
 
 
-def pack_body(
-    counts, gates, hidden, upstream, near, far, own, scales, counts_s, gates_v, hidden_v, sems
-):
+def pack_body(counts, gates, hidden, upstream, grads, *refs):
+    n_cuts = len(CUTS)
+    near, far, own, scales, *pieces = refs[: 4 + n_cuts]
+    counts_s, gates_v, hidden_v, pieces_v, sems, piece_sems, out_sems = refs[4 + n_cuts :]
     cap = own.shape[0]
     wide = upstream.shape[1]
+    count, _, width = pieces_v.shape
     sources = (
         (counts, counts_s),
         (gates, gates_v),
@@ -49,7 +51,13 @@
         pltpu.make_async_copy(source, target, sems.at[index])
         for index, (source, target) in enumerate(sources)
     ]
-    for load in loads:
+    piece_loads = [
+        pltpu.make_async_copy(
+            grads.at[:, pl.ds(s * width, width)], pieces_v.at[s], piece_sems.at[s]
+        )
+        for s in range(count)
+    ]
+    for load in loads + piece_loads:
         load.start()
     for load in loads:
         load.wait()
@@ -66,32 +74,16 @@
         else:
             out[...] = scaled
         scales[span, :] = jnp.broadcast_to(scale, (cap, 128))
-
-
-def split_body(grads, *refs):
-    pieces, (pieces_v, load_sems, store_sems) = refs[: len(CUTS)], refs[len(CUTS) :]
-    count, _, width = pieces_v.shape
-    loads = [
-        pltpu.make_async_copy(
-            grads.at[:, pl.ds(s * width, width)], pieces_v.at[s], load_sems.at[s]
-        )
-        for s in range(count)
-    ]
+    for load in piece_loads:
+        load.wait()
     stores = [
         pltpu.make_async_copy(
-            pieces_v.at[s, pl.ds(first, size), :],
-            pieces[index].at[s],
-            store_sems.at[s * len(CUTS) + index],
+            pieces_v.at[:, pl.ds(first, size), :], pieces[index], out_sems.at[index]
         )
-        for s in range(count)
         for index, (first, size) in enumerate(CUTS)
     ]
-    for load in loads:
-        load.start()
-    for s, load in enumerate(loads):
-        load.wait()
-        for store in stores[s * len(CUTS) : (s + 1) * len(CUTS)]:
-            store.start()
+    for store in stores:
+        store.start()
     for store in stores:
         store.wait()
 
@@ -249,37 +241,33 @@
     def shape(*dims, kind=bf16):
         return jax.ShapeDtypeStruct(dims, kind)
 
-    near, far, own, scales = call(
+    near, far, own, scales, *pieces = pl.pallas_call(
         pack_body,
-        [shape(cap, wide + hid)] * 2 + [shape(cap, hid), shape(rows, 128, kind=f32)],
-        [HBM] * 4,
+        out_shape=[shape(cap, wide + hid)] * 2
+        + [shape(cap, hid), shape(rows, 128, kind=f32)]
+        + [pltpu.HBM((n_seq, size, width), bf16) for _, size in CUTS],
+        in_specs=[HBM] * 5,
+        out_specs=[VMEM] * 4 + [HBM] * len(CUTS),
         scratch_shapes=[
             pltpu.SMEM((1, 3), jnp.int32),
             pltpu.VMEM((1, rows), f32),
             pltpu.VMEM((rows, hid), bf16),
+            pltpu.VMEM((n_seq, tokens, width), bf16),
             pltpu.SemaphoreType.DMA((5,)),
+            pltpu.SemaphoreType.DMA((n_seq,)),
+            pltpu.SemaphoreType.DMA((len(CUTS),)),
         ],
+        compiler_params=pltpu.CompilerParams(vmem_limit_bytes=12 * 1024 * 1024),
         name="pack",
     )(
         in_hbm(row_counts),
         in_hbm(row_gates.reshape(1, rows)),
         in_hbm(hidden_rows),
         in_hbm(upstream_rows),
+        in_hbm(output_grad.reshape(tokens, n_seq * width)),
     )
     near = shifted(near, "exp", -step)
     far = shifted(far, "exp", -2 * step)
-    pieces = call(
-        split_body,
-        [pltpu.HBM((n_seq, size, width), bf16) for _, size in CUTS],
-        [HBM],
-        outs=HBM,
-        scratch_shapes=[
-            pltpu.VMEM((n_seq, tokens, width), bf16),
-            pltpu.SemaphoreType.DMA((n_seq,)),
-            pltpu.SemaphoreType.DMA((n_seq * len(CUTS),)),
-        ],
-        name="split",
-    )(in_hbm(output_grad.reshape(tokens, n_seq * width)))
     head_grads = []
     for piece in pieces:
         head_grads.append(

time: 88.4 us -> 81.5 us (0.922)
  the two profiles are of different devices: /device:TPU:4 before, /device:TPU:128 now
where the time goes in v4:
time: 81.5 us; the launch traced here: 81.1 us
  starting transfers between devices  25.4 us (31%)
  waiting for transfers between devices  22.8 us (28%)
  blocking collectives  17.2 us (21%)
  Pallas kernels  14 us (17%)
    ppermute x2, starting transfers between devices, shifted(): return lax.ppermute(block, axis, route)  20.6 us
    all_to_all x1, blocking collectives, on_device(): lax.all_to_all(parts.reshape(n_seq, own_rows, hid), 'seq', split_axis=0,...  17.2 us
    all_to_all x1, waiting for transfers between devices, on_device(): lax.all_to_all(piece, 'seq', split_axis=0, concat_axis=0, tiled=True)  12.2 us
    ppermute x2, waiting for transfers between devices, shifted(): return lax.ppermute(block, axis, route)  10.6 us
    pallas_call x1, Pallas kernels, on_device(): call(probs_body, pltpu.HBM((heads, seq_len, seq_len), bf16), [HBM, HBM, H...  5.61 us
    all_to_all x1, starting transfers between devices, on_device(): lax.all_to_all(piece, 'seq', split_axis=0, concat_axis=0, tiled=True)  3.49 us
    pallas_call x1, Pallas kernels, on_device(): call(value_body, shape(seq_len, width), [HBM] + [VMEM] * len(CUTS), scrat...  3.17 us
    pallas_call x1, Pallas kernels, on_device(): pl.pallas_call(pack_body, out_shape=[shape(cap, wide + hid)] * 2 + [shape...  2.43 us
  transfers between devices with their start and end apart: 5, of which 3 were waited for; matrix products, arithmetic and copies ran while one was open for 1% of the time, Pallas kernels for 9%

profile of v4, /device:TPU:128, one launch (start us, length us, event | category | flops | bytes accessed | tf_op | source)
XLA Modules:
  0.0 81.1 jit_solution(5140736956109919526)
XLA Ops:
  0.6 0.0 copy-start
  0.6 0.0 copy-start.1
  0.7 2.4 %pack.1 = (bf16[64,1408]{1,0:T(8,128)(2,1)S(1)}, bf16[64,1408]{1,0:T(8,128)(2,1)S(1)}, bf16[64,512]{1,0:T(8,128)(2,1)S(1)}, f32[192,128]{1,0:T(8,128)S(1)}, bf16[8,128,256]{2,1,0:T(8,128)(2,1)}) custom-call(s32[1,3]{1,0:T(1,128)} %counts.1, f32[1,192]{1,0:T(1,128)} %bitcast.17, bf16[192,512]{1,0:T(8,128)(2,1)} %hidden.1, bf16[192,896]{1,0:T(8,128)(2,1)} %upstream.5, ...), custom_call_target="tpu_custom_call" | custom-call | tf_op jit(solution)/shard_map/pack/pallas_call | solution.py:244
  3.1 18.7 %collective-permute-start = (bf16[64,1408]{1,0:T(8,128)(2,1)S(1)}, bf16[64,1408]{1,0:T(8,128)(2,1)S(1)}, u32[]{:S(2)}, u32[]{:S(2)}) collective-permute-start(bf16[64,1408]{1,0:T(8,128)(2,1)S(1)} %get-tuple-element.11), channel_id=1, source_target_pairs={{0,704},{32,736},{64,768},{96,800},{128,832},{160,864},{192,896},{... | collective-permute-start | bytes 540680 | tf_op jit(solution)/shard_map/ppermute | solution.py:216
  21.8 1.9 %collective-permute-start.1 = (bf16[64,1408]{1,0:T(8,128)(2,1)S(1)}, bf16[64,1408]{1,0:T(8,128)(2,1)S(1)}, u32[]{:S(2)}, u32[]{:S(2)}) collective-permute-start(bf16[64,1408]{1,0:T(8,128)(2,1)S(1)} %get-tuple-element.12), channel_id=1, source_target_pairs={{0,384},{32,416},{64,448},{96,480},{128,512},{160,544},{192,576},{... | collective-permute-start | bytes 540680 | tf_op jit(solution)/shard_map/ppermute | solution.py:216
  23.7 5.6 %probs.1 = bf16[2,1024,1024]{2,1,0:T(8,128)(2,1)} custom-call(bf16[1024,512]{1,0:T(8,128)(2,1)} %bitcast.11, bf16[512,256]{1,0:T(8,128)(2,1)} %bitcast.16, bf16[1024,256]{1,0:T(8,128)(2,1)} %bitcast.13), custom_call_target="tpu_custom_call" | custom-call | tf_op jit(solution)/shard_map/probs/pallas_call | solution.py:279
  29.3 4.0 %collective-permute-done.near = bf16[64,1408]{1,0:T(8,128)(2,1)S(1)} collective-permute-done((bf16[64,1408]{1,0:T(8,128)(2,1)S(1)}, bf16[64,1408]{1,0:T(8,128)(2,1)S(1)}, u32[]{:S(2)}, u32[]{:S(2)}) %collective-permute-start) | collective-permute-done | bytes 180256 | tf_op jit(solution)/shard_map/ppermute | solution.py:216
  33.4 6.6 %collective-permute-done.1.far = bf16[64,1408]{1,0:T(8,128)(2,1)S(1)} collective-permute-done((bf16[64,1408]{1,0:T(8,128)(2,1)S(1)}, bf16[64,1408]{1,0:T(8,128)(2,1)S(1)}, u32[]{:S(2)}, u32[]{:S(2)}) %collective-permute-start.1) | collective-permute-done | bytes 180256 | tf_op jit(solution)/shard_map/ppermute | solution.py:216
  40.0 0.0 copy-done
  40.0 0.0 copy-done.1
  40.0 1.0 %parts.1 = bf16[192,512]{1,0:T(8,128)(2,1)S(1)} custom-call(bf16[512,896]{1,0:T(8,128)(2,1)S(1)} %bitcast.9, bf16[192,896]{1,0:T(8,128)(2,1)S(1)} %copy-done, bf16[64,1408]{1,0:T(8,128)(2,1)S(1)} %collective-permute-done.near, bf16[64,1408]{1,0:T(8,128)(2,1)S(1)} %collective-permute-done.1.far), custom_call_target="tpu_custom_call" | custom-call | tf_op jit(solution)/shard_map/parts/pallas_call | solution.py:302
  41.0 17.2 %all_to_all.10 = bf16[8,24,512]{2,1,0:T(8,128)(2,1)S(1)} all-to-all(bf16[8,24,512]{2,1,0:T(8,128)(2,1)S(1)} %bitcast.10), channel_id=1, replica_groups=mesh['exp'=32,'seq'=8,'dp'=4] {'seq'}, dimensions={0} | all-to-all | bytes 393216 | tf_op jit(solution)/shard_map/all_to_all | solution.py:305
  58.2 3.5 %all-to-all-start = ((bf16[8,128,256]{2,1,0:T(8,128)(2,1)}), bf16[8,128,256]{2,1,0:T(8,128)(2,1)S(1)}, u32[]{:S(2)}, u32[]{:S(2)}) async-start(bf16[8,128,256]{2,1,0:T(8,128)(2,1)} %get-tuple-element.14), calls=%async_computation | async-start | bytes 1048576 | tf_op jit(solution)/shard_map/all_to_all | solution.py:274
  61.7 0.7 collective-permute-start.3
  62.4 0.7 collective-permute-start.2
  63.1 0.1 dynamic-slice_reduce_fusion
  63.2 1.8 %weight.1 = bf16[512,896]{1,0:T(8,128)(2,1)} custom-call(bf16[192,896]{1,0:T(8,128)(2,1)S(1)} %copy-done, bf16[64,512]{1,0:T(8,128)(2,1)S(1)} %get-tuple-element.18.own, bf16[64,1408]{1,0:T(8,128)(2,1)S(1)} %collective-permute-done.near, bf16[64,1408]{1,0:T(8,128)(2,1)S(1)} %collective-permute-done.1.far), custom_call_target="tpu_custom_call" | custom-call | tf_op jit(solution)/shard_map/weight/pallas_call | solution.py:308
  65.1 0.0 collective-permute-done.3
  65.1 0.0 collective-permute-done.2
  65.1 0.7 select_multiply_fusion
  65.8 12.2 %all-to-all-done.refs_0_ = bf16[8,128,256]{2,1,0:T(8,128)(2,1)S(1)} async-done(((bf16[8,128,256]{2,1,0:T(8,128)(2,1)}), bf16[8,128,256]{2,1,0:T(8,128)(2,1)S(1)}, u32[]{:S(2)}, u32[]{:S(2)}) %all-to-all-start) | async-done | bytes 524320 | tf_op jit(solution)/shard_map/all_to_all | solution.py:274
  77.9 3.2 %value.1 = bf16[1024,256]{1,0:T(8,128)(2,1)} custom-call(bf16[2,1024,1024]{2,1,0:T(8,128)(2,1)} %probs.1, bf16[8,128,256]{2,1,0:T(8,128)(2,1)S(1)} %all-to-all-done.refs_0_), custom_call_target="tpu_custom_call" | custom-call | tf_op jit(solution)/shard_map/value/pallas_call | solution.py:311
  (3 shorter events, 0.1 us)
Async XLA Ops:
  0.6 39.4 %copy-start = (bf16[192,896]{1,0:T(8,128)(2,1)S(1)}, bf16[192,896]{1,0:T(8,128)(2,1)}, u32[]{:S(2)}) copy-start(bf16[192,896]{1,0:T(8,128)(2,1)} %upstream.5) | copy-start | bytes 1032196
  0.6 39.3 %copy-start.1 = (bf16[1,512,896]{2,1,0:T(8,128)(2,1)S(1)}, bf16[1,512,896]{2,1,0:T(8,128)(2,1)}, u32[]{:S(2)}) copy-start(bf16[1,512,896]{2,1,0:T(8,128)(2,1)} %param.13) | copy-start | bytes 2752516
  3.1 30.3 %collective-permute-start = (bf16[64,1408]{1,0:T(8,128)(2,1)S(1)}, bf16[64,1408]{1,0:T(8,128)(2,1)S(1)}, u32[]{:S(2)}, u32[]{:S(2)}) collective-permute-start(bf16[64,1408]{1,0:T(8,128)(2,1)S(1)} %get-tuple-element.11), channel_id=1, source_target_pairs={{0,704},{32,736},{64,768},{96,800},{128,832},{160,864},{192,896},{... | collective-permute-start | bytes 540680 | tf_op jit(solution)/shard_map/ppermute | solution.py:216
  21.8 18.2 %collective-permute-start.1 = (bf16[64,1408]{1,0:T(8,128)(2,1)S(1)}, bf16[64,1408]{1,0:T(8,128)(2,1)S(1)}, u32[]{:S(2)}, u32[]{:S(2)}) collective-permute-start(bf16[64,1408]{1,0:T(8,128)(2,1)S(1)} %get-tuple-element.12), channel_id=1, source_target_pairs={{0,384},{32,416},{64,448},{96,480},{128,512},{160,544},{192,576},{... | collective-permute-start | bytes 540680 | tf_op jit(solution)/shard_map/ppermute | solution.py:216
  58.2 19.7 %all-to-all-start = ((bf16[8,128,256]{2,1,0:T(8,128)(2,1)}), bf16[8,128,256]{2,1,0:T(8,128)(2,1)S(1)}, u32[]{:S(2)}, u32[]{:S(2)}) async-start(bf16[8,128,256]{2,1,0:T(8,128)(2,1)} %get-tuple-element.14), calls=%async_computation | async-start | bytes 1048576 | tf_op jit(solution)/shard_map/all_to_all | solution.py:274
  61.7 3.3 %collective-permute-start.3 = (bf16[24,512]{1,0:T(8,128)(2,1)S(1)}, bf16[24,512]{1,0:T(8,128)(2,1)S(1)}, u32[]{:S(2)}, u32[]{:S(2)}) collective-permute-start(bf16[24,512]{1,0:T(8,128)(2,1)S(1)} %convert_element_type.14), channel_id=1, source_target_pairs={{8,328},{40,360},{72,392},{104,424},{136,456},{168,488},{200,520},... | collective-permute-start | bytes 73736 | tf_op jit(solution)/shard_map/ppermute | solution.py:336
  62.4 2.6 %collective-permute-start.2 = (bf16[24,512]{1,0:T(8,128)(2,1)S(1)}, bf16[24,512]{1,0:T(8,128)(2,1)S(1)}, u32[]{:S(2)}, u32[]{:S(2)}) collective-permute-start(bf16[24,512]{1,0:T(8,128)(2,1)S(1)} %convert_element_type.14), channel_id=1, source_target_pairs={{20,660},{52,692},{84,724},{116,756},{148,788},{180,820},{212,852}... | collective-permute-start | bytes 73736 | tf_op jit(solution)/shard_map/ppermute | solution.py:336
